TPU v7x, 32 devices: a whole 2x2x4 slice. The times are simulated.
32 devices in a mesh: parts: 2 (over y), turn: 4 (over x, core), branch: 4 (over z).
Axes of the slice: x: 2, y: 2, z: 4, core: 2. Of those that a mesh axis runs over, the one named last changes fastest.
Arguments:
- query: bfloat16 [4096, 4096], P(('parts', 'turn', 'branch')), parts along dimension 0, may hold values from -128 to 128
- branch_key_value: bfloat16 [2, 4096, 512], P(None, ('parts', 'turn', 'branch')), parts along dimension 1, may hold values from -4 to 4
- turn_key_value: bfloat16 [2, 64, 512], P(None, ('parts', 'turn', 'branch')), parts along dimension 1, may hold values from -4 to 4
- kv_trunk: bfloat16 [2, 32, 512], P(None, ('parts', 'turn', 'branch')), parts along dimension 1, may hold values from -4 to 4
- grad_out: bfloat16 [4096, 4096], P(('parts', 'turn', 'branch')), parts along dimension 0, may hold values from -6 to 6
- branch_lengths: int32 [32, 4], P(('parts', 'turn', 'branch')), parts along dimension 0, may hold values from 1 to 64, 128 in all within a row
- parents: int32 [8], P('parts'), parts along dimension 0, may hold values from -1 to 2, as said below
Outputs:
- attended: bfloat16 [4096, 4096], P(('parts', 'turn', 'branch')), parts along dimension 0
- grad_query: bfloat16 [4096, 4096], P(('parts', 'turn', 'branch')), parts along dimension 0
- grad_branch_kv: bfloat16 [2, 4096, 512], P(None, ('parts', 'turn', 'branch')), parts along dimension 1
- grad_turn_kv: bfloat16 [2, 64, 512], P(None, ('parts', 'turn', 'branch')), parts along dimension 1
- grad_trunk_kv: bfloat16 [2, 32, 512], P(None, ('parts', 'turn', 'branch')), parts along dimension 1
There are 2 independent parts, one for each index of `parts`. A program takes and returns all parts, laid end to end along the dimension named above; each array names one. Nothing has to cross between parts.
Inputs may be any that keep to these rules, and one draw needn't show every extreme that they name: parents[t] is -1 or a turn before t; parents[0] is -1 and the last turn's parent is the turn before it.
All inputs are finite; a program needn't handle non-finite values.
Results may differ from a plain program's by a relative error of at most 0.02.
Values may be sent and summed in bfloat16 or wider, within the bound.
No kernel may reach another device: no remote copies, remote signals or barrier semaphores. Data moves between devices by JAX's collectives and lax.ppermute only.
A program may use at most 64 MiB of HBM per device.

v0:
```python
import math

import jax
import jax.numpy as jnp
from jax import lax
from jax.sharding import PartitionSpec as P

QUERY_HEADS = 32
KEY_VALUE_HEADS = 4
HEAD_SIZE = 128
QUERY_PER_KEY = 8


masked_score = -1e30


def ancestry(parents, turn_count):
    position = jnp.arange(turn_count, dtype=jnp.int32)
    parent_of = parents[:, None] == position[None, :]
    start = position[:, None] == position[None, :]

    def widen(sweep, reached):
        return reached | jnp.any(reached[:, :, None] & parent_of[None, :, :], axis=1)

    return lax.fori_loop(0, turn_count, widen, start)


def visible(path_row, lengths, trunk_rows, turn_rows, turn_count, branch_rows):
    turn_length = turn_rows // turn_count
    owner_turn = jnp.arange(turn_rows, dtype=jnp.int32) // turn_length
    on_path = jnp.any(
        (owner_turn[:, None] == jnp.arange(turn_count, dtype=jnp.int32)[None, :])
        & path_row[None, :],
        axis=1,
    )
    segment_ends = jnp.cumsum(lengths, dtype=jnp.int32)
    position = jnp.arange(branch_rows, dtype=jnp.int32)
    segment = jnp.sum((position[:, None] >= segment_ends[None, :]).astype(jnp.int32), axis=1)
    inside = (segment[:, None] == segment[None, :]) & (position[None, :] <= position[:, None])
    leading = jnp.ones((branch_rows, trunk_rows), dtype=bool)
    middle = jnp.broadcast_to(on_path[None, :], (branch_rows, turn_rows))
    return jnp.concatenate([leading, middle, inside], axis=1)


def group_terms(query, key_rows, values, grad_out, allowed, group_index):
    query_total = query.shape[0]
    group_width = QUERY_PER_KEY * HEAD_SIZE
    softmax_scale = 1.0 / math.sqrt(HEAD_SIZE)
    start = group_index * group_width
    queries = lax.dynamic_slice_in_dim(query, start, group_width, 1).reshape(
        query_total, QUERY_PER_KEY, HEAD_SIZE
    )
    cotangent = lax.dynamic_slice_in_dim(grad_out, start, group_width, 1).reshape(
        query_total, QUERY_PER_KEY, HEAD_SIZE
    )
    head_keys = lax.dynamic_slice_in_dim(key_rows, group_index * HEAD_SIZE, HEAD_SIZE, 1)
    head_values = lax.dynamic_slice_in_dim(values, group_index * HEAD_SIZE, HEAD_SIZE, 1)
    scores = (
        jnp.einsum("rgd,kd->grk", queries, head_keys, preferred_element_type=jnp.float32)
        * softmax_scale
    )
    scores = jnp.where(allowed[None, :, :], scores, masked_score)
    largest = jnp.max(scores, axis=2, keepdims=True)
    exponent = jnp.exp(scores - largest)
    probs = exponent / jnp.sum(exponent, axis=2, keepdims=True)
    rounded = probs.astype(jnp.bfloat16)
    attended = jnp.einsum(
        "grk,kd->rgd", rounded, head_values, preferred_element_type=jnp.float32
    ).astype(jnp.bfloat16)
    delta = jnp.sum(cotangent.astype(jnp.float32) * attended.astype(jnp.float32), axis=2)
    dprob = jnp.einsum("rgd,kd->grk", cotangent, head_values, preferred_element_type=jnp.float32)
    dscore = (probs * (dprob - jnp.transpose(delta)[:, :, None])).astype(jnp.bfloat16)
    grad_query = (
        jnp.einsum("grk,kd->rgd", dscore, head_keys, preferred_element_type=jnp.float32)
        * softmax_scale
    ).astype(jnp.bfloat16)
    grad_keys = (
        jnp.einsum("grk,rgd->kd", dscore, queries, preferred_element_type=jnp.float32)
        * softmax_scale
    )
    grad_values = jnp.einsum("grk,rgd->kd", rounded, cotangent, preferred_element_type=jnp.float32)
    return (
        attended.reshape(query_total, group_width),
        grad_query.reshape(query_total, group_width),
        grad_keys,
        grad_values,
    )


def device_terms(query, key_rows, values, grad_out, allowed):
    query_total = query.shape[0]
    key_total = key_rows.shape[0]
    group_width = QUERY_PER_KEY * HEAD_SIZE

    def single_group(group_index, totals):
        attended, grad_query, grad_keys, grad_values = totals
        piece_out, piece_query, piece_keys, piece_values = group_terms(
            query, key_rows, values, grad_out, allowed, group_index
        )
        attended = lax.dynamic_update_slice_in_dim(
            attended, piece_out, group_index * group_width, 1
        )
        grad_query = lax.dynamic_update_slice_in_dim(
            grad_query, piece_query, group_index * group_width, 1
        )
        grad_keys = lax.dynamic_update_slice_in_dim(
            grad_keys, piece_keys, group_index * HEAD_SIZE, 1
        )
        grad_values = lax.dynamic_update_slice_in_dim(
            grad_values, piece_values, group_index * HEAD_SIZE, 1
        )
        return (attended, grad_query, grad_keys, grad_values)

    initial_state = (
        jnp.zeros((query_total, QUERY_HEADS * HEAD_SIZE), jnp.bfloat16),
        jnp.zeros((query_total, QUERY_HEADS * HEAD_SIZE), jnp.bfloat16),
        jnp.zeros((key_total, KEY_VALUE_HEADS * HEAD_SIZE), jnp.float32),
        jnp.zeros((key_total, KEY_VALUE_HEADS * HEAD_SIZE), jnp.float32),
    )
    return lax.fori_loop(0, KEY_VALUE_HEADS, single_group, initial_state)


def on_device(query, branch_key_value, turn_key_value, kv_trunk, grad_out, branch_lengths, parents):
    turn_count = lax.axis_size("turn")
    nearby = (
        lax.all_gather(kv_trunk, "branch", axis=1, tiled=True),
        lax.all_gather(turn_key_value, "branch", axis=1, tiled=True),
    )
    trunk_all, turn_all = (
        lax.all_gather(nearby[0], "turn", axis=1, tiled=True),
        lax.all_gather(nearby[1], "turn", axis=1, tiled=True),
    )
    reached = ancestry(parents, turn_count)
    turn_index = lax.axis_index("turn")
    path_row = jnp.any(
        reached & (jnp.arange(turn_count, dtype=jnp.int32)[:, None] == turn_index), axis=0
    )
    trunk_rows = trunk_all.shape[1]
    turn_rows = turn_all.shape[1]
    shared_rows = trunk_rows + turn_rows
    allowed = visible(
        path_row, branch_lengths[0], trunk_rows, turn_rows, turn_count, query.shape[0]
    )
    key_rows = jnp.concatenate([trunk_all[0], turn_all[0], branch_key_value[0]], axis=0)
    value_rows = jnp.concatenate([trunk_all[1], turn_all[1], branch_key_value[1]], axis=0)
    attended, grad_query, grad_keys, grad_values = device_terms(
        query, key_rows, value_rows, grad_out, allowed
    )
    grad_trunk = jnp.stack([grad_keys[:trunk_rows], grad_values[:trunk_rows]])
    grad_turn = jnp.stack([grad_keys[trunk_rows:shared_rows], grad_values[trunk_rows:shared_rows]])
    grad_branch = jnp.stack([grad_keys[shared_rows:], grad_values[shared_rows:]]).astype(
        jnp.bfloat16
    )
    sum_trunk, sum_turn = (
        lax.psum_scatter(grad_trunk, ("turn", "branch"), scatter_dimension=1, tiled=True),
        lax.psum_scatter(grad_turn, ("turn", "branch"), scatter_dimension=1, tiled=True),
    )
    return (
        attended,
        grad_query,
        grad_branch,
        sum_turn.astype(jnp.bfloat16),
        sum_trunk.astype(jnp.bfloat16),
    )


def solution(mesh):
    return jax.shard_map(
        on_device,
        mesh=mesh,
        in_specs=(
            P(("parts", "turn", "branch"), None),
            P(None, ("parts", "turn", "branch"), None),
            P(None, ("parts", "turn", "branch"), None),
            P(None, ("parts", "turn", "branch"), None),
            P(("parts", "turn", "branch"), None),
            P(("parts", "turn", "branch"), None),
            P("parts"),
        ),
        out_specs=(
            P(("parts", "turn", "branch"), None),
            P(("parts", "turn", "branch"), None),
            P(None, ("parts", "turn", "branch"), None),
            P(None, ("parts", "turn", "branch"), None),
            P(None, ("parts", "turn", "branch"), None),
        ),
        check_vma=False,
    )
```

profile of v0, /device:TPU:0, one launch (start us, length us, event | category | flops | bytes accessed | tf_op | source)
XLA Modules:
  0.0 157.0 jit_solution(16002256091089100070)
XLA Ops:
  0.7 0.6 copy-done.13
  1.3 0.6 dynamic-slice
  2.6 0.6 copy-done.11
  3.2 0.2 reduce-window.8
  3.5 0.6 copy-done.12
  4.1 0.8 while.31
  5.2 0.4 copy-done.9
  5.6 0.7 copy-done.10
  6.3 13.6 %all_gather.12 = bf16[2,4,512]{2,0,1:T(2,128)(2,1)S(1)} all-gather(bf16[2,1,512]{2,0,1:T(2,128)(2,1)S(1)} %copy-done.10), channel_id=1, replica_groups=mesh['parts'=2,'turn'=4,'branch'=4] {'branch'}, dimensions={1}, use_global_device_ids=true | all-gather | bytes 10240 | tf_op jit(solution)/shard_map/all_gather | solution.py:126
  19.9 13.2 %all_gather.14 = bf16[2,8,512]{2,0,1:T(2,128)(2,1)S(1)} all-gather(bf16[2,2,512]{2,0,1:T(2,128)(2,1)S(1)} %copy.56), channel_id=1, replica_groups=mesh['parts'=2,'turn'=4,'branch'=4] {'branch'}, dimensions={1}, use_global_device_ids=true | all-gather | bytes 20480 | tf_op jit(solution)/shard_map/all_gather | solution.py:127
  33.3 5.2 %all_gather.13 = bf16[2,16,512]{2,0,1:T(2,128)(2,1)S(1)} all-gather(bf16[2,4,512]{2,0,1:T(2,128)(2,1)S(1)} %all_gather.12), channel_id=1, replica_groups=mesh['parts'=2,'turn'=4,'branch'=4] {'turn'}, dimensions={1}, use_global_device_ids=true | all-gather | bytes 40960 | tf_op jit(solution)/shard_map/all_gather | solution.py:130
  38.6 5.2 %all_gather.15 = bf16[2,32,512]{2,1,0:T(8,128)(2,1)S(1)} all-gather(bf16[2,8,512]{2,1,0:T(8,128)(2,1)S(1)} %copy.57), channel_id=1, replica_groups=mesh['parts'=2,'turn'=4,'branch'=4] {'turn'}, dimensions={1}, use_global_device_ids=true | all-gather | bytes 81920 | tf_op jit(solution)/shard_map/all_gather | solution.py:131
  43.9 0.8 broadcast.77.clone
  44.6 0.8 broadcast.77
  45.6 43.4 %while.30 = (s32[]{:T(128)}, bf16[128,4096]{1,0:T(8,128)(2,1)S(1)}, bf16[128,4096]{1,0:T(8,128)(2,1)S(1)}, f32[176,512]{1,0:T(8,128)}, f32[176,512]{1,0:T(8,128)...) while((s32[]{:T(128)}, bf16[128,4096]{1,0:T(8,128)(2,1)S(1)}, ...), condition=%wide.region_11.12_spmd, body=%wide.region_7.11_spmd.sunk | while | flops 373284352 | bytes 12505477 | solution.py:120
  45.7 1.1 constant_dynamic-slice_fusion.4
  46.8 0.2 copy.86
  46.9 1.0 constant_dynamic-slice_fusion.5
  47.9 0.2 copy.87
  48.1 1.2 fusion.100
  49.3 0.5 multiply_reduce_fusion.2
  49.9 1.4 fusion.101
  51.4 2.0 %fusion.104 = f32[176,512]{1,0:T(8,128)} fusion(f32[176,512]{1,0:T(8,128)} %get-tuple-element.449, s32[]{:T(128)S(6)} %select_n.65, bf16[128,8,128]{0,2,1:T(8,128)(2,1)S(1)} %bitcast.177, f32[8,128]{1,0:T(8,128)S(1)} %get-tuple-element.408, bf16[128,8,128]{0,2,1:T(8,128)(2,1)S(1)} %bitcast.173, pred[128,176]{0,1:T(8,128)(4,1)S(1)} %get-tuple-element.467, ...), kind=kOutput, calls=%fused_computation.15.clone.1 | convolution fusion | flops 93177008 | bytes 687104 | tf_op jit(solution)/shard_map/while/body/eval_jaxpr/grk,rgd->kd/dot_general | solution.py:81
  53.4 0.9 fusion.103
  54.3 1.0 fusion.102
  55.6 0.8 copy-done.5
  56.5 1.1 constant_dynamic-slice_fusion.4
  57.6 0.2 copy.86
  57.8 1.0 constant_dynamic-slice_fusion.5
  58.8 0.2 copy.87
  58.9 1.2 fusion.100
  60.2 0.5 multiply_reduce_fusion.2
  60.7 1.4 fusion.101
  62.3 2.0 %fusion.104 = f32[176,512]{1,0:T(8,128)} fusion(f32[176,512]{1,0:T(8,128)} %get-tuple-element.449, s32[]{:T(128)S(6)} %select_n.65, bf16[128,8,128]{0,2,1:T(8,128)(2,1)S(1)} %bitcast.177, f32[8,128]{1,0:T(8,128)S(1)} %get-tuple-element.408, bf16[128,8,128]{0,2,1:T(8,128)(2,1)S(1)} %bitcast.173, pred[128,176]{0,1:T(8,128)(4,1)S(1)} %get-tuple-element.467, ...), kind=kOutput, calls=%fused_computation.15.clone.1 | convolution fusion | flops 93177008 | bytes 687104 | tf_op jit(solution)/shard_map/while/body/eval_jaxpr/grk,rgd->kd/dot_general | solution.py:81
  64.2 0.9 fusion.103
  65.1 1.0 fusion.102
  66.4 0.8 copy-done.5
  67.3 1.1 constant_dynamic-slice_fusion.4
  68.4 0.2 copy.86
  68.6 1.0 constant_dynamic-slice_fusion.5
  69.6 0.2 copy.87
  69.8 1.2 fusion.100
  71.0 0.5 multiply_reduce_fusion.2
  71.5 1.4 fusion.101
  73.1 2.0 %fusion.104 = f32[176,512]{1,0:T(8,128)} fusion(f32[176,512]{1,0:T(8,128)} %get-tuple-element.449, s32[]{:T(128)S(6)} %select_n.65, bf16[128,8,128]{0,2,1:T(8,128)(2,1)S(1)} %bitcast.177, f32[8,128]{1,0:T(8,128)S(1)} %get-tuple-element.408, bf16[128,8,128]{0,2,1:T(8,128)(2,1)S(1)} %bitcast.173, pred[128,176]{0,1:T(8,128)(4,1)S(1)} %get-tuple-element.467, ...), kind=kOutput, calls=%fused_computation.15.clone.1 | convolution fusion | flops 93177008 | bytes 687104 | tf_op jit(solution)/shard_map/while/body/eval_jaxpr/grk,rgd->kd/dot_general | solution.py:81
  75.1 0.9 fusion.103
  76.0 1.0 fusion.102
  77.2 0.8 copy-done.5
  78.2 1.1 constant_dynamic-slice_fusion.4
  79.3 0.2 copy.86
  79.4 1.0 constant_dynamic-slice_fusion.5
  80.6 1.2 fusion.100
  81.8 0.5 multiply_reduce_fusion.2
  82.4 1.4 fusion.101
  83.9 2.0 %fusion.104 = f32[176,512]{1,0:T(8,128)} fusion(f32[176,512]{1,0:T(8,128)} %get-tuple-element.449, s32[]{:T(128)S(6)} %select_n.65, bf16[128,8,128]{0,2,1:T(8,128)(2,1)S(1)} %bitcast.177, f32[8,128]{1,0:T(8,128)S(1)} %get-tuple-element.408, bf16[128,8,128]{0,2,1:T(8,128)(2,1)S(1)} %bitcast.173, pred[128,176]{0,1:T(8,128)(4,1)S(1)} %get-tuple-element.467, ...), kind=kOutput, calls=%fused_computation.15.clone.1 | convolution fusion | flops 93177008 | bytes 687104 | tf_op jit(solution)/shard_map/while/body/eval_jaxpr/grk,rgd->kd/dot_general | solution.py:81
  85.9 0.9 fusion.103
  86.8 1.0 fusion.102
  88.0 0.8 copy-done.5
  89.0 0.9 slice_bitcast_fusion.6
  89.8 0.8 slice_bitcast_fusion.7
  90.9 0.7 pad_maximum_fusion
  91.6 63.5 %all-reduce.4 = (bf16[2,32,512]{2,1,0:T(8,128)(2,1)S(1)}, bf16[2,16,512]{2,0,1:T(2,128)(2,1)S(1)}) all-reduce(f32[2,32,512]{2,1,0:T(8,128)S(1)} %pad_maximum_fusion.3, f32[2,16,512]{2,0,1:T(2,128)S(1)} %copy.61), channel_id=2, replica_groups=mesh['parts'=2,'turn'=4,'branch'=4] {'turn','branch'}, use_global_device_ids=true, to_apply=%region_12.13.clone | all-reduce | flops 49152 | bytes 294912
  155.2 0.6 dynamic-slice_convert_fusion
  155.8 1.2 dynamic-slice_convert_fusion.1
  (95 shorter events, 3.8 us)
Async XLA Ops:
  0.6 0.7 copy-start.13
  2.6 0.7 copy-start.11
  3.5 0.7 copy-start.12
  4.9 0.7 copy-start.9
  5.6 0.7 copy-start.10
  33.2 10.6 %copy-start.6 = (bf16[2,128,512]{2,1,0:T(8,128)(2,1)S(1)}, bf16[2,128,512]{2,1,0:T(8,128)(2,1)}, u32[]{:S(2)}) copy-start(bf16[2,128,512]{2,1,0:T(8,128)(2,1)} %param.12) | copy-start | bytes 786436
  45.6 3.7 %copy-start.4 = (bf16[176,512]{1,0:T(8,128)(2,1)}, bf16[176,512]{1,0:T(8,128)(2,1)S(1)}, u32[]{:S(2)}) copy-start(bf16[176,512]{1,0:T(8,128)(2,1)S(1)} %get-tuple-element.468) | copy-start | bytes 540676 | tf_op jit(solution)/shard_map/while
  45.6 3.7 %copy-start.7 = (bf16[176,512]{1,0:T(8,128)(2,1)}, bf16[176,512]{1,0:T(8,128)(2,1)S(1)}, u32[]{:S(2)}) copy-start(bf16[176,512]{1,0:T(8,128)(2,1)S(1)} %get-tuple-element.466) | copy-start | bytes 540676 | tf_op jit(solution)/shard_map/while
  55.5 0.9 copy-start.5
  55.5 1.0 copy-start.8
  56.5 3.7 %copy-start.4 = (bf16[176,512]{1,0:T(8,128)(2,1)}, bf16[176,512]{1,0:T(8,128)(2,1)S(1)}, u32[]{:S(2)}) copy-start(bf16[176,512]{1,0:T(8,128)(2,1)S(1)} %get-tuple-element.468) | copy-start | bytes 540676 | tf_op jit(solution)/shard_map/while
  56.5 3.7 %copy-start.7 = (bf16[176,512]{1,0:T(8,128)(2,1)}, bf16[176,512]{1,0:T(8,128)(2,1)S(1)}, u32[]{:S(2)}) copy-start(bf16[176,512]{1,0:T(8,128)(2,1)S(1)} %get-tuple-element.466) | copy-start | bytes 540676 | tf_op jit(solution)/shard_map/while
  66.3 0.9 copy-start.5
  66.3 1.0 copy-start.8
  67.3 3.7 %copy-start.4 = (bf16[176,512]{1,0:T(8,128)(2,1)}, bf16[176,512]{1,0:T(8,128)(2,1)S(1)}, u32[]{:S(2)}) copy-start(bf16[176,512]{1,0:T(8,128)(2,1)S(1)} %get-tuple-element.468) | copy-start | bytes 540676 | tf_op jit(solution)/shard_map/while
  67.3 3.7 %copy-start.7 = (bf16[176,512]{1,0:T(8,128)(2,1)}, bf16[176,512]{1,0:T(8,128)(2,1)S(1)}, u32[]{:S(2)}) copy-start(bf16[176,512]{1,0:T(8,128)(2,1)S(1)} %get-tuple-element.466) | copy-start | bytes 540676 | tf_op jit(solution)/shard_map/while
  77.1 0.9 copy-start.5
  77.2 1.0 copy-start.8
  78.2 3.7 %copy-start.4 = (bf16[176,512]{1,0:T(8,128)(2,1)}, bf16[176,512]{1,0:T(8,128)(2,1)S(1)}, u32[]{:S(2)}) copy-start(bf16[176,512]{1,0:T(8,128)(2,1)S(1)} %get-tuple-element.468) | copy-start | bytes 540676 | tf_op jit(solution)/shard_map/while
  78.2 3.7 %copy-start.7 = (bf16[176,512]{1,0:T(8,128)(2,1)}, bf16[176,512]{1,0:T(8,128)(2,1)S(1)}, u32[]{:S(2)}) copy-start(bf16[176,512]{1,0:T(8,128)(2,1)S(1)} %get-tuple-element.466) | copy-start | bytes 540676 | tf_op jit(solution)/shard_map/while
  88.0 0.9 copy-start.5
  88.0 1.0 copy-start.8
  89.0 66.2 %copy-start = (bf16[128,4096]{1,0:T(8,128)(2,1)}, bf16[128,4096]{1,0:T(8,128)(2,1)S(1)}, u32[]{:S(2)}) copy-start(bf16[128,4096]{1,0:T(8,128)(2,1)S(1)} %get-tuple-element.279) | copy-start | bytes 3145732
  89.0 66.2 %copy-start.1 = (bf16[128,4096]{1,0:T(8,128)(2,1)}, bf16[128,4096]{1,0:T(8,128)(2,1)S(1)}, u32[]{:S(2)}) copy-start(bf16[128,4096]{1,0:T(8,128)(2,1)S(1)} %get-tuple-element.278) | copy-start | bytes 3145732
  89.0 1.8 %copy-start.2 = (f32[176,512]{1,0:T(8,128)S(1)}, f32[176,512]{1,0:T(8,128)}, u32[]{:S(2)}) copy-start(f32[176,512]{1,0:T(8,128)} %get-tuple-element.198) | copy-start | bytes 1081348
  89.8 1.0 copy-start.3
where the time goes:
time: 158 us; the launch traced here: 157 us
  blocking collectives  101 us (64%)
  matrix products  28.2 us (18%)
  local copies, waits for them, and re-layouts  23.9 us (15%)
  other arithmetic  2.21 us (1%)
    unnamed x1, blocking collectives  63.5 us
    all_gather x1, blocking collectives, on_device(): lax.all_gather(kv_trunk, 'branch', axis=1, tiled=True)  13.6 us
    all_gather x1, blocking collectives, on_device(): lax.all_gather(turn_key_value, 'branch', axis=1, tiled=True)  13.2 us
    dot_general x4, matrix products, group_terms(): jnp.einsum('grk,rgd->kd', rounded, cotangent, preferred_element_type=jnp....  7.87 us
    dot_general x4, matrix products, group_terms(): jnp.einsum('rgd,kd->grk', cotangent, head_values, preferred_element_type=...  5.57 us
    all_gather x1, blocking collectives, on_device(): lax.all_gather(nearby[1], 'turn', axis=1, tiled=True)  5.24 us
    all_gather x1, blocking collectives, on_device(): lax.all_gather(nearby[0], 'turn', axis=1, tiled=True)  5.19 us
    dynamic_slice x8, local copies, waits for them, and re-layouts, group_terms(): lax.dynamic_slice_in_dim(grad_out, start, group_width, 1)  5.05 us

commit v1 on v0

v1 whole, which is shorter than its diff:
```python
import functools
import math

import jax
import jax.numpy as jnp
from jax import lax
from jax.experimental import pallas as pl
from jax.experimental.pallas import tpu as pltpu
from jax.sharding import PartitionSpec as P

HEAD_SIZE = 128
masked_score = -1e30


def exchange_steps(mesh):
    steps = []
    for axis in ("branch", "turn"):
        size = mesh.shape[axis]
        assert size & (size - 1) == 0
        bit = size // 2
        while bit:
            steps.append((axis, bit, size))
            bit //= 2
    return steps


def swap(x, axis, bit, size):
    return lax.ppermute(x, axis, [(i, i ^ bit) for i in range(size)])


def kernel(
    steps, trunk_rows, turn_rows, turns, parents_ref, lengths_ref, q_ref, kv_ref, shared_ref,
    do_ref, out_ref, dq_ref, dkv_ref, keep_ref, send_ref, bias_ref, w_ref, ds_ref,
):
    group = pl.program_id(0)
    queries = q_ref.shape[0]
    slots = shared_ref.shape[0]
    rows = trunk_rows + turn_rows
    shared = slots * rows
    features = kv_ref.shape[2] * pl.num_programs(0)
    heads = q_ref.shape[1] // HEAD_SIZE
    scale = 1.0 / math.sqrt(HEAD_SIZE)
    f32 = jnp.float32
    bf16 = jnp.bfloat16

    @pl.when(group == 0)
    def _():
        me = lax.axis_index("turn")
        slot = lax.broadcasted_iota(jnp.int32, (slots, queries), 0)
        away = jnp.zeros_like(slot)
        for k, (axis, bit, _) in enumerate(steps):
            if axis == "turn":
                away = away + ((slot >> k) & 1) * bit
        owner = jnp.bitwise_xor(away, me)
        path = owner == me
        at = me
        for _ in range(turns - 1):
            at = jnp.where(at >= 0, parents_ref[jnp.maximum(at, 0)], -1)
            path = path | (owner == at)
        turn_bias = jnp.where(path, 0.0, masked_score).astype(f32)
        for r in range(rows):
            piece = jnp.zeros_like(turn_bias) if r < trunk_rows else turn_bias
            bias_ref[r * slots:(r + 1) * slots, :] = piece
        key_at = lax.broadcasted_iota(jnp.int32, (queries, queries), 0)
        query_at = lax.broadcasted_iota(jnp.int32, (queries, queries), 1)
        first = jnp.zeros_like(query_at)
        end = jnp.int32(0)
        for c in range(lengths_ref.shape[1]):
            end = end + lengths_ref[0, c]
            first = jnp.where(query_at >= end, end, first)
        inside = (key_at >= first) & (key_at <= query_at)
        bias_ref[shared:, :] = jnp.where(inside, 0.0, masked_score).astype(f32)

    lane = pl.multiple_of(group * HEAD_SIZE, HEAD_SIZE)

    def gathered(part):
        pieces = [
            shared_ref[:, pl.ds((2 * r + part) * features + lane, HEAD_SIZE)] for r in range(rows)
        ]
        return jnp.concatenate(pieces + [kv_ref[part]], axis=0)

    keys, values = gathered(0), gathered(1)
    keys_t = keys.T
    values_t = values.T
    per = 2 if heads % 2 == 0 else 1
    bias = jnp.concatenate([bias_ref[...]] * per, axis=1)
    nt = (((1,), (1,)), ((), ()))
    nn = (((1,), (0,)), ((), ()))

    def stacked(ref, lo, hi):
        return jnp.concatenate(
            [ref[:, h * HEAD_SIZE:(h + 1) * HEAD_SIZE] for h in range(lo, hi)], axis=0
        )

    def unstack(ref, lo, value):
        turned = value.T
        for h in range(per):
            ref[:, (lo + h) * HEAD_SIZE:(lo + h + 1) * HEAD_SIZE] = turned[
                h * queries:(h + 1) * queries, :
            ]

    for lo in range(0, heads, per):
        q = stacked(q_ref, lo, lo + per)
        do = stacked(do_ref, lo, lo + per)
        s = lax.dot_general(keys, q, nt, preferred_element_type=f32) + bias
        top = jnp.max(s, axis=0, keepdims=True)
        e = jnp.exp((s - top) * scale)
        p = e * (1.0 / jnp.sum(e, axis=0, keepdims=True))
        w = p.astype(bf16)
        dp = lax.dot_general(values, do, nt, preferred_element_type=f32)
        delta = jnp.sum(p * dp, axis=0, keepdims=True)
        ds = (p * (dp - delta)).astype(bf16)
        span = slice(lo * queries, (lo + per) * queries)
        w_ref[:, span] = w
        ds_ref[:, span] = ds
        o_t = lax.dot_general(values_t, w, nn, preferred_element_type=f32)
        unstack(out_ref, lo, o_t.astype(bf16))
        dq_t = lax.dot_general(keys_t, ds, nn, preferred_element_type=f32) * scale
        unstack(dq_ref, lo, dq_t.astype(bf16))

    dk = lax.dot_general(
        ds_ref[...], stacked(q_ref, 0, heads), nn, preferred_element_type=f32
    ) * scale
    dv = lax.dot_general(w_ref[...], stacked(do_ref, 0, heads), nn, preferred_element_type=f32)
    dkv_ref[0] = dk[shared:].astype(bf16)
    dkv_ref[1] = dv[shared:].astype(bf16)
    half = slots // 2
    for part, grad in ((0, dk), (1, dv)):
        for r in range(rows):
            at_lane = pl.ds((2 * r + part) * features + lane, HEAD_SIZE)
            keep_ref[:, at_lane] = grad[r * slots:r * slots + half]
            send_ref[:, at_lane] = grad[r * slots + half:(r + 1) * slots].astype(bf16)


def on_device(mesh, query, branch_kv, turn_kv, trunk_kv, grad_out, lengths, parents):
    steps = exchange_steps(mesh)
    slots = 2 ** len(steps)
    queries, width = query.shape
    features = branch_kv.shape[2]
    groups = features // HEAD_SIZE
    trunk_rows, turn_rows = trunk_kv.shape[1], turn_kv.shape[1]
    rows = trunk_rows + turn_rows
    flat = rows * 2 * features

    own = jnp.concatenate([trunk_kv, turn_kv], axis=1)
    held = jnp.swapaxes(own, 0, 1).reshape(1, flat)
    for axis, bit, size in steps:
        held = jnp.concatenate([held, swap(held, axis, bit, size)], axis=0)

    bf16 = jnp.bfloat16
    key_rows = slots * rows + queries
    block = pl.BlockSpec((queries, width // groups), lambda g: (0, g))
    kv_block = pl.BlockSpec((2, queries, HEAD_SIZE), lambda g: (0, 0, g))
    whole = lambda n: pl.BlockSpec((n, flat), lambda g: (0, 0))
    smem = pl.BlockSpec(memory_space=pltpu.SMEM)
    attended, grad_query, grad_branch, keep, send = pl.pallas_call(
        functools.partial(kernel, steps, trunk_rows, turn_rows, mesh.shape["turn"]),
        grid=(groups,),
        in_specs=[smem, smem, block, kv_block, whole(slots), block],
        out_specs=[block, block, kv_block, whole(slots // 2), whole(slots // 2)],
        out_shape=[
            jax.ShapeDtypeStruct(query.shape, bf16),
            jax.ShapeDtypeStruct(query.shape, bf16),
            jax.ShapeDtypeStruct(branch_kv.shape, bf16),
            jax.ShapeDtypeStruct((slots // 2, flat), jnp.float32),
            jax.ShapeDtypeStruct((slots // 2, flat), bf16),
        ],
        scratch_shapes=[
            pltpu.VMEM((key_rows, queries), jnp.float32),
            pltpu.VMEM((key_rows, queries * (width // features)), bf16),
            pltpu.VMEM((key_rows, queries * (width // features)), bf16),
        ],
        name="tree_attention",
    )(parents, lengths, query, branch_kv, held, grad_out)

    total = keep
    for k in reversed(range(len(steps))):
        axis, bit, size = steps[k]
        if k < len(steps) - 1:
            half = total.shape[0] // 2
            send, total = total[half:].astype(bf16), total[:half]
        total = total + swap(send, axis, bit, size).astype(jnp.float32)
    total = jnp.swapaxes(total.astype(bf16).reshape(rows, 2, features), 0, 1)
    return attended, grad_query, grad_branch, total[:, trunk_rows:], total[:, :trunk_rows]


def solution(mesh):
    everywhere = ("parts", "turn", "branch")
    by_row = P(everywhere, None)
    by_middle = P(None, everywhere, None)
    return jax.shard_map(
        functools.partial(on_device, mesh),
        mesh=mesh,
        in_specs=(by_row, by_middle, by_middle, by_middle, by_row, by_row, P("parts")),
        out_specs=(by_row, by_row, by_middle, by_middle, by_middle),
        check_vma=False,
    )
```

time: 158 us -> 42.4 us (0.27)
  blocking collectives: 101 us -> 0 us
  matrix products: 28.2 us -> 0 us
  local copies, waits for them, and re-layouts: 23.9 us -> 3.27 us
  starting transfers between devices: 0 us -> 15.1 us
  waiting for transfers between devices: 0 us -> 13.4 us
  Pallas kernels: 0 us -> 8.46 us
    unnamed x1 -> x0, blocking collectives: 63.5 us -> none
    all_gather x4 -> x0, blocking collectives: 37.3 us -> none  [the longest x1 13.6 us: on_device(): lax.all_gather(kv_trunk, 'branch', axis=1, tiled=True)]
    dot_general x20 -> x0, matrix products: 23.3 us -> none  [the longest x4 7.87 us: group_terms(): jnp.einsum('grk,rgd->kd', rounded, cotangent, preferred_element_type=jnp....]
    ppermute x0 -> x8, starting transfers between devices: none -> 15.1 us  [swap(): return lax.ppermute(x, axis, [(i, i ^ bit) for i in range(size)])]
    ppermute x0 -> x8, waiting for transfers between devices: none -> 13.4 us  [swap(): return lax.ppermute(x, axis, [(i, i ^ bit) for i in range(size)])]
    dynamic_slice x16 -> x0, local copies, waits for them, and re-layouts: 9.62 us -> none  [the longest x8 5.05 us: group_terms(): lax.dynamic_slice_in_dim(grad_out, start, group_width, 1)]
    pallas_call x0 -> x1, Pallas kernels: none -> 8.46 us  [on_device(): pl.pallas_call(functools.partial(kernel, steps, trunk_rows, turn_rows, me...]
    sub x4 -> x0, matrix products: 4.87 us -> none  [group_terms(): exponent = jnp.exp(scores - largest)]
  transfers between devices with their start and end apart: 0 -> 8, of which waited for: 0 -> 8; matrix products, arithmetic and copies ran while one was open for 0% -> 0% of each run, Pallas kernels for 0% -> 0%
where the time goes in v1:
time: 42.4 us; the launch traced here: 42.1 us
  starting transfers between devices  15.1 us (36%)
  waiting for transfers between devices  13.4 us (32%)
  Pallas kernels  8.46 us (20%)
  local copies, waits for them, and re-layouts  3.27 us (8%)
  other arithmetic  1.14 us (3%)
  between operations  0.72 us (2%)
    ppermute x8, starting transfers between devices, swap(): return lax.ppermute(x, axis, [(i, i ^ bit) for i in range(size)])  15.1 us
    ppermute x8, waiting for transfers between devices, swap(): return lax.ppermute(x, axis, [(i, i ^ bit) for i in range(size)])  13.4 us
    pallas_call x1, Pallas kernels, on_device(): pl.pallas_call(functools.partial(kernel, steps, trunk_rows, turn_rows, me...  8.46 us
    concatenate x1, local copies, waits for them, and re-layouts, on_device(): held = jnp.concatenate([held, swap(held, axis, bit, size)], axis=0)  1.3 us
    unnamed x4, local copies, waits for them, and re-layouts  1.29 us
    add x3, other arithmetic, on_device(): total = total + swap(send, axis, bit, size).astype(jnp.float32)  0.93 us
  transfers between devices with their start and end apart: 8, of which 8 were waited for; matrix products, arithmetic and copies ran while one was open for 0% of the time, Pallas kernels for 0%

profile of v1, /device:TPU:0, one launch (start us, length us, event | category | flops | bytes accessed | tf_op | source)
XLA Modules:
  0.0 42.1 jit_solution(13764380453566225970)
XLA Ops:
  0.6 0.0 copy-start
  0.6 0.7 %copy.12 = bf16[2,1,512]{2,1,0:T(2,128)(2,1)S(1)} copy(bf16[2,1,512]{2,0,1:T(2,128)(2,1)} %param.10) | data formatting | bytes 4096 | tf_op args[3]
  1.3 0.0 copy-done
  1.4 4.1 %collective-permute-start = (bf16[1,3072]{1,0:T(2,128)(2,1)S(1)}, bf16[1,3072]{1,0:T(2,128)(2,1)S(1)}, u32[]{:S(2)}, u32[]{:S(2)}) collective-permute-start(bf16[1,3072]{1,0:T(2,128)(2,1)S(1)} %reshape.16), channel_id=1, source_target_pairs={{0,2},{1,3},{2,0},{3,1},{4,6},{5,7},{6,4},{7,5},{8,10},{9,11},{10,... | collective-permute-start | bytes 18440 | tf_op jit(solution)/shard_map/ppermute | solution.py:28
  5.5 1.7 %collective-permute-done = bf16[1,3072]{1,0:T(2,128)(2,1)S(1)} collective-permute-done((bf16[1,3072]{1,0:T(2,128)(2,1)S(1)}, bf16[1,3072]{1,0:T(2,128)(2,1)S(1)}, u32[]{:S(2)}, u32[]{:S(2)}) %collective-permute-start) | collective-permute-done | bytes 6176 | tf_op jit(solution)/shard_map/ppermute | solution.py:28
  7.2 2.0 %collective-permute-start.1 = (bf16[2,3072]{1,0:T(2,128)(2,1)S(1)}, bf16[2,3072]{1,0:T(2,128)(2,1)S(1)}, u32[]{:S(2)}, u32[]{:S(2)}) collective-permute-start(bf16[2,3072]{1,0:T(2,128)(2,1)S(1)} %pad_maximum_fusion.2), channel_id=1, source_target_pairs={{0,1},{1,0},{2,3},{3,2},{4,5},{5,4},{6,7},{7,6},{8,9},{9,8},{10,11... | collective-permute-start | bytes 36872 | tf_op jit(solution)/shard_map/ppermute | solution.py:28
  9.2 1.8 %collective-permute-done.1 = bf16[2,3072]{1,0:T(2,128)(2,1)S(1)} collective-permute-done((bf16[2,3072]{1,0:T(2,128)(2,1)S(1)}, bf16[2,3072]{1,0:T(2,128)(2,1)S(1)}, u32[]{:S(2)}, u32[]{:S(2)}) %collective-permute-start.1) | collective-permute-done | bytes 12320 | tf_op jit(solution)/shard_map/ppermute | solution.py:28
  11.0 1.9 %collective-permute-start.2 = (bf16[4,3072]{1,0:T(4,128)(2,1)S(1)}, bf16[4,3072]{1,0:T(4,128)(2,1)S(1)}, u32[]{:S(2)}, u32[]{:S(2)}) collective-permute-start(bf16[4,3072]{1,0:T(4,128)(2,1)S(1)} %pad_maximum_fusion.1), channel_id=1, source_target_pairs={{0,8},{4,12},{8,0},{12,4},{1,9},{5,13},{9,1},{13,5},{2,10},{6,14},... | collective-permute-start | bytes 73736 | tf_op jit(solution)/shard_map/ppermute | solution.py:28
  12.9 2.0 %collective-permute-done.2 = bf16[4,3072]{1,0:T(4,128)(2,1)S(1)} collective-permute-done((bf16[4,3072]{1,0:T(4,128)(2,1)S(1)}, bf16[4,3072]{1,0:T(4,128)(2,1)S(1)}, u32[]{:S(2)}, u32[]{:S(2)}) %collective-permute-start.2) | collective-permute-done | bytes 24608 | tf_op jit(solution)/shard_map/ppermute | solution.py:28
  14.9 0.1 pad_maximum_fusion
  15.0 0.1 collective-permute-start.3
  15.1 1.2 %collective-permute-done.3 = bf16[8,3072]{1,0:T(8,128)(2,1)S(1)} collective-permute-done((bf16[8,3072]{1,0:T(8,128)(2,1)S(1)}, bf16[8,3072]{1,0:T(8,128)(2,1)S(1)}, u32[]{:S(2)}, u32[]{:S(2)}) %collective-permute-start.3) | collective-permute-done | bytes 49184 | tf_op jit(solution)/shard_map/ppermute | solution.py:28
  16.3 1.3 %concatenate.22.shared_ref = bf16[16,3072]{1,0:T(8,128)(2,1)} concatenate(bf16[1,3072]{1,0:T(2,128)(2,1)S(1)} %reshape.16, bf16[1,3072]{1,0:T(2,128)(2,1)S(1)} %collective-permute-done, bf16[2,3072]{1,0:T(2,128)(2,1)S(1)} %collective-permute-done.1, bf16[4,3072]{1,0:T(4,128)(2,1)S(1)} %collective-permute-done.2, bf16[8,3072]{1,0:T(8,128)(2,1)S(1)} %collective-permute-done.3), dimensions={0} | concatenate | bytes 196608 | tf_op jit(solution)/shard_map/concatenate | solution.py:148
  17.6 8.5 %tree_attention.1 = (bf16[128,4096]{1,0:T(8,128)(2,1)}, bf16[128,4096]{1,0:T(8,128)(2,1)}, bf16[2,128,512]{2,1,0:T(8,128)(2,1)}, f32[8,3072]{1,0:T(8,128)}, bf16[8,3072]{1,0:T(8,128)(2,1)}) custom-call(s32[4]{0:T(128)} %parents_ref.1, s32[1,4]{1,0:T(1,128)} %lengths_ref.1, bf16[128,4096]{1,0:T(8,128)(2,1)} %q_ref.1, bf16[2,128,512]{2,1,0:T(8,128)(2,1)} %kv_ref.1, ...), custom_call_target="tpu_custom_call" | custom-call | tf_op jit(solution)/shard_map/tree_attention/pallas_call | solution.py:156
  26.1 0.2 collective-permute-start.4
  26.3 1.3 %collective-permute-done.4 = bf16[8,3072]{1,0:T(8,128)(2,1)S(1)} collective-permute-done((bf16[8,3072]{1,0:T(8,128)(2,1)}, bf16[8,3072]{1,0:T(8,128)(2,1)S(1)}, u32[]{:S(2)}, u32[]{:S(2)}) %collective-permute-start.4) | collective-permute-done | bytes 49184 | tf_op jit(solution)/shard_map/ppermute | solution.py:28
  27.6 0.9 %convert_add_fusion = f32[8,3072]{1,0:T(8,128)S(1)} fusion(f32[8,3072]{1,0:T(8,128)} %get-tuple-element.13, bf16[8,3072]{1,0:T(8,128)(2,1)S(1)} %collective-permute-done.4), kind=kLoop, calls=%fused_computation | loop fusion | flops 49152 | bytes 245760 | tf_op jit(solution)/shard_map/add | solution.py:182
  28.5 1.9 %collective-permute-start.5 = (bf16[4,3072]{1,0:T(4,128)(2,1)S(1)}, bf16[4,3072]{1,0:T(4,128)(2,1)S(1)}, u32[]{:S(2)}, u32[]{:S(2)}) collective-permute-start(bf16[4,3072]{1,0:T(4,128)(2,1)S(1)} %slice.53), channel_id=1, source_target_pairs={{0,8},{4,12},{8,0},{12,4},{1,9},{5,13},{9,1},{13,5},{2,10},{6,14},... | collective-permute-start | bytes 73736 | tf_op jit(solution)/shard_map/ppermute | solution.py:28
  30.4 2.0 %collective-permute-done.5 = bf16[4,3072]{1,0:T(4,128)(2,1)S(1)} collective-permute-done((bf16[4,3072]{1,0:T(4,128)(2,1)S(1)}, bf16[4,3072]{1,0:T(4,128)(2,1)S(1)}, u32[]{:S(2)}, u32[]{:S(2)}) %collective-permute-start.5) | collective-permute-done | bytes 24608 | tf_op jit(solution)/shard_map/ppermute | solution.py:28
  32.4 2.0 %collective-permute-start.6 = (bf16[2,3072]{1,0:T(2,128)(2,1)S(1)}, bf16[2,3072]{1,0:T(2,128)(2,1)S(1)}, u32[]{:S(2)}, u32[]{:S(2)}) collective-permute-start(bf16[2,3072]{1,0:T(2,128)(2,1)S(1)} %slice.54), channel_id=1, source_target_pairs={{0,1},{1,0},{2,3},{3,2},{4,5},{5,4},{6,7},{7,6},{8,9},{9,8},{10,11... | collective-permute-start | bytes 36872 | tf_op jit(solution)/shard_map/ppermute | solution.py:28
  34.4 1.8 %collective-permute-done.6 = bf16[2,3072]{1,0:T(2,128)(2,1)S(1)} collective-permute-done((bf16[2,3072]{1,0:T(2,128)(2,1)S(1)}, bf16[2,3072]{1,0:T(2,128)(2,1)S(1)}, u32[]{:S(2)}, u32[]{:S(2)}) %collective-permute-start.6) | collective-permute-done | bytes 12320 | tf_op jit(solution)/shard_map/ppermute | solution.py:28
  36.2 3.0 %collective-permute-start.7 = (bf16[1,3072]{1,0:T(2,128)(2,1)S(1)}, bf16[1,3072]{1,0:T(2,128)(2,1)S(1)}, u32[]{:S(2)}, u32[]{:S(2)}) collective-permute-start(bf16[1,3072]{1,0:T(2,128)(2,1)S(1)} %slice.55), channel_id=1, source_target_pairs={{0,2},{1,3},{2,0},{3,1},{4,6},{5,7},{6,4},{7,5},{8,10},{9,11},{10,... | collective-permute-start | bytes 18440 | tf_op jit(solution)/shard_map/ppermute | solution.py:28
  39.2 1.7 %collective-permute-done.7 = bf16[1,3072]{1,0:T(2,128)(2,1)S(1)} collective-permute-done((bf16[1,3072]{1,0:T(2,128)(2,1)S(1)}, bf16[1,3072]{1,0:T(2,128)(2,1)S(1)}, u32[]{:S(2)}, u32[]{:S(2)}) %collective-permute-start.7) | collective-permute-done | bytes 6176 | tf_op jit(solution)/shard_map/ppermute | solution.py:28
  41.0 0.6 %slice.42 = bf16[2,1,512]{2,0,1:T(2,128)(2,1)} slice(bf16[2,3,512]{2,0,1:T(2,128)(2,1)S(1)} %bitcast.3), slice={[0:2], [0:1], [0:512]} | slice | bytes 4096 | tf_op jit(solution)/shard_map/slice | solution.py:184
  41.5 0.6 %copy.14 = bf16[2,2,512]{2,1,0:T(2,128)(2,1)} copy(bf16[2,2,512]{2,0,1:T(2,128)(2,1)S(1)} %slice.41) | data formatting | bytes 8192
  (13 shorter events, 0.3 us)
Async XLA Ops:
  0.6 0.7 %copy-start = (bf16[2,2,512]{2,1,0:T(2,128)(2,1)S(1)}, bf16[2,2,512]{2,1,0:T(2,128)(2,1)}, u32[]{:S(2)}) copy-start(bf16[2,2,512]{2,1,0:T(2,128)(2,1)} %param.9) | copy-start | bytes 12292
  1.4 5.8 %collective-permute-start = (bf16[1,3072]{1,0:T(2,128)(2,1)S(1)}, bf16[1,3072]{1,0:T(2,128)(2,1)S(1)}, u32[]{:S(2)}, u32[]{:S(2)}) collective-permute-start(bf16[1,3072]{1,0:T(2,128)(2,1)S(1)} %reshape.16), channel_id=1, source_target_pairs={{0,2},{1,3},{2,0},{3,1},{4,6},{5,7},{6,4},{7,5},{8,10},{9,11},{10,... | collective-permute-start | bytes 18440 | tf_op jit(solution)/shard_map/ppermute | solution.py:28
  7.2 3.8 %collective-permute-start.1 = (bf16[2,3072]{1,0:T(2,128)(2,1)S(1)}, bf16[2,3072]{1,0:T(2,128)(2,1)S(1)}, u32[]{:S(2)}, u32[]{:S(2)}) collective-permute-start(bf16[2,3072]{1,0:T(2,128)(2,1)S(1)} %pad_maximum_fusion.2), channel_id=1, source_target_pairs={{0,1},{1,0},{2,3},{3,2},{4,5},{5,4},{6,7},{7,6},{8,9},{9,8},{10,11... | collective-permute-start | bytes 36872 | tf_op jit(solution)/shard_map/ppermute | solution.py:28
  11.0 3.9 %collective-permute-start.2 = (bf16[4,3072]{1,0:T(4,128)(2,1)S(1)}, bf16[4,3072]{1,0:T(4,128)(2,1)S(1)}, u32[]{:S(2)}, u32[]{:S(2)}) collective-permute-start(bf16[4,3072]{1,0:T(4,128)(2,1)S(1)} %pad_maximum_fusion.1), channel_id=1, source_target_pairs={{0,8},{4,12},{8,0},{12,4},{1,9},{5,13},{9,1},{13,5},{2,10},{6,14},... | collective-permute-start | bytes 73736 | tf_op jit(solution)/shard_map/ppermute | solution.py:28
  15.0 1.3 %collective-permute-start.3 = (bf16[8,3072]{1,0:T(8,128)(2,1)S(1)}, bf16[8,3072]{1,0:T(8,128)(2,1)S(1)}, u32[]{:S(2)}, u32[]{:S(2)}) collective-permute-start(bf16[8,3072]{1,0:T(8,128)(2,1)S(1)} %pad_maximum_fusion), channel_id=1, source_target_pairs={{0,4},{4,0},{8,12},{12,8},{1,5},{5,1},{9,13},{13,9},{2,6},{6,2},{1... | collective-permute-start | bytes 147464 | tf_op jit(solution)/shard_map/ppermute | solution.py:28
  26.1 1.5 %collective-permute-start.4 = (bf16[8,3072]{1,0:T(8,128)(2,1)}, bf16[8,3072]{1,0:T(8,128)(2,1)S(1)}, u32[]{:S(2)}, u32[]{:S(2)}) collective-permute-start(bf16[8,3072]{1,0:T(8,128)(2,1)} %get-tuple-element.14), channel_id=1, source_target_pairs={{0,4},{4,0},{8,12},{12,8},{1,5},{5,1},{9,13},{13,9},{2,6},{6,2},{1... | collective-permute-start | bytes 147464 | tf_op jit(solution)/shard_map/ppermute | solution.py:28
  28.5 3.9 %collective-permute-start.5 = (bf16[4,3072]{1,0:T(4,128)(2,1)S(1)}, bf16[4,3072]{1,0:T(4,128)(2,1)S(1)}, u32[]{:S(2)}, u32[]{:S(2)}) collective-permute-start(bf16[4,3072]{1,0:T(4,128)(2,1)S(1)} %slice.53), channel_id=1, source_target_pairs={{0,8},{4,12},{8,0},{12,4},{1,9},{5,13},{9,1},{13,5},{2,10},{6,14},... | collective-permute-start | bytes 73736 | tf_op jit(solution)/shard_map/ppermute | solution.py:28
  32.4 3.8 %collective-permute-start.6 = (bf16[2,3072]{1,0:T(2,128)(2,1)S(1)}, bf16[2,3072]{1,0:T(2,128)(2,1)S(1)}, u32[]{:S(2)}, u32[]{:S(2)}) collective-permute-start(bf16[2,3072]{1,0:T(2,128)(2,1)S(1)} %slice.54), channel_id=1, source_target_pairs={{0,1},{1,0},{2,3},{3,2},{4,5},{5,4},{6,7},{7,6},{8,9},{9,8},{10,11... | collective-permute-start | bytes 36872 | tf_op jit(solution)/shard_map/ppermute | solution.py:28
  36.2 4.7 %collective-permute-start.7 = (bf16[1,3072]{1,0:T(2,128)(2,1)S(1)}, bf16[1,3072]{1,0:T(2,128)(2,1)S(1)}, u32[]{:S(2)}, u32[]{:S(2)}) collective-permute-start(bf16[1,3072]{1,0:T(2,128)(2,1)S(1)} %slice.55), channel_id=1, source_target_pairs={{0,2},{1,3},{2,0},{3,1},{4,6},{5,7},{6,4},{7,5},{8,10},{9,11},{10,... | collective-permute-start | bytes 18440 | tf_op jit(solution)/shard_map/ppermute | solution.py:28

commit v2 on v1

v2 whole, which is shorter than its diff:
```python
import functools
import math

import jax
import jax.numpy as jnp
from jax import lax
from jax.experimental import pallas as pl
from jax.experimental.pallas import tpu as pltpu
from jax.sharding import PartitionSpec as P


HEAD_SIZE = 128
masked_score = -1e30
softmax_scale = 1.0 / math.sqrt(HEAD_SIZE)
exp2_scale = softmax_scale * math.log2(math.e)
f32 = jnp.float32
bf16 = jnp.bfloat16
NT = (((1,), (1,)), ((), ()))
NN = (((1,), (0,)), ((), ()))
vmem = pl.BlockSpec(memory_space=pltpu.VMEM)
smem = pl.BlockSpec(memory_space=pltpu.SMEM)


def exchange_steps(mesh):
    steps = []
    for axis in ("branch", "turn"):
        size = mesh.shape[axis]
        assert size & (size - 1) == 0
        bit = size // 2
        while bit:
            steps.append((axis, bit, size))
            bit //= 2
    return steps


def swap(x, step):
    axis, bit, size = step
    return lax.ppermute(x, axis, [(i, i ^ bit) for i in range(size)])


def dot(a, b, dims):
    return lax.dot_general(a, b, dims, preferred_element_type=f32)


def stacked(ref, lo, hi):
    return jnp.concatenate(
        [ref[:, h * HEAD_SIZE:(h + 1) * HEAD_SIZE] for h in range(lo, hi)], axis=0
    )


def head_chunks(first, last, per_group, per):
    for group in range(first, last):
        for lo in range(group * per_group, (group + 1) * per_group, per):
            yield group, lo


def own_kernel(first_group, per_group, per, lengths_ref, q_ref, do_ref, kv_ref, e_ref, dp_ref, stat_ref):
    queries = q_ref.shape[0]
    groups = e_ref.shape[1] // (queries * per_group)
    key_at = lax.broadcasted_iota(jnp.int32, (queries, queries), 0)
    query_at = lax.broadcasted_iota(jnp.int32, (queries, queries), 1)
    start = jnp.zeros_like(query_at)
    end = jnp.int32(0)
    for c in range(lengths_ref.shape[1]):
        end = end + lengths_ref[0, c]
        start = jnp.where(query_at >= end, end, start)
    inside = (key_at >= start) & (key_at <= query_at)
    bias = jnp.where(inside, 0.0, masked_score).astype(f32)
    bias = jnp.concatenate([bias] * per, axis=1)
    base = first_group * per_group
    for group, lo in head_chunks(first_group, first_group + groups, per_group, per):
        lanes = slice(group * HEAD_SIZE, (group + 1) * HEAD_SIZE)
        span = slice((lo - base) * queries, (lo - base + per) * queries)
        s = dot(kv_ref[0, :, lanes], stacked(q_ref, lo, lo + per), NT) + bias
        top = jnp.max(s, axis=0, keepdims=True)
        e = jnp.exp2((s - top) * exp2_scale)
        dp = dot(kv_ref[1, :, lanes], stacked(do_ref, lo, lo + per), NT)
        e_ref[:, span] = e
        dp_ref[:, span] = dp
        stat_ref[0:1, span] = top
        stat_ref[1:2, span] = jnp.sum(e, axis=0, keepdims=True)
        stat_ref[2:3, span] = jnp.sum(e * dp, axis=0, keepdims=True)


def shared_rows_of(shared_ref, rows, features, part, group):
    return jnp.concatenate(
        [
            shared_ref[:, pl.ds((2 * r + part) * features + group * HEAD_SIZE, HEAD_SIZE)]
            for r in range(rows)
        ],
        axis=0,
    )


def shared_kernel(
    steps, trunk_rows, turn_rows, turns, per_group, per, parts, parents_ref, near_ref, far_ref, q_ref, do_ref, *refs
):
    stat_refs, refs = refs[:parts], refs[parts:]
    shared_ref, w_ref, ds_ref, joined_ref, keep_ref, send_ref = refs
    queries = q_ref.shape[0]
    slots = shared_ref.shape[0]
    shared_ref[:slots // 2] = near_ref[...]
    shared_ref[slots // 2:] = far_ref[...]
    rows = trunk_rows + turn_rows
    features = shared_ref.shape[1] // (2 * rows)
    groups = features // HEAD_SIZE
    half = slots // 2

    me = lax.axis_index("turn")
    slot = lax.broadcasted_iota(jnp.int32, (slots, per * queries), 0)
    away = jnp.zeros_like(slot)
    for k, (axis, bit, _) in enumerate(steps):
        if axis == "turn":
            away = away + ((slot >> k) & 1) * bit
    owner = jnp.bitwise_xor(away, me)
    path = owner == me
    at = me
    for _ in range(turns - 1):
        at = jnp.where(at >= 0, parents_ref[jnp.maximum(at, 0)], -1)
        path = path | (owner == at)
    turn_bias = jnp.where(path, 0.0, masked_score).astype(f32)
    bias = jnp.concatenate(
        [jnp.zeros_like(turn_bias)] * trunk_rows + [turn_bias] * turn_rows, axis=0
    )

    for group in range(groups):
        keys = shared_rows_of(shared_ref, rows, features, 0, group)
        values = shared_rows_of(shared_ref, rows, features, 1, group)
        first, last = group * per_group, (group + 1) * per_group
        for lo in range(first, last, per):
            span = slice(lo * queries, (lo + per) * queries)
            part, place = divmod(lo, groups * per_group // parts)
            stat_ref = stat_refs[part]
            stat = slice(place * queries, (place + per) * queries)
            own_top = stat_ref[0:1, stat]
            s = dot(keys, stacked(q_ref, lo, lo + per), NT) + bias
            top = jnp.maximum(jnp.max(s, axis=0, keepdims=True), own_top)
            e = jnp.exp2((s - top) * exp2_scale)
            shrink = jnp.exp2((own_top - top) * exp2_scale)
            dp = dot(values, stacked(do_ref, lo, lo + per), NT)
            total = jnp.sum(e, axis=0, keepdims=True) + shrink * stat_ref[1:2, stat]
            inverse = 1.0 / total
            delta = inverse * (
                jnp.sum(e * dp, axis=0, keepdims=True) + shrink * stat_ref[2:3, stat]
            )
            p = e * inverse
            w_ref[:, span] = p.astype(bf16)
            ds_ref[:, span] = (p * (dp - delta)).astype(bf16)
            joined_ref[0:1, span] = shrink * inverse
            joined_ref[1:2, span] = delta
        span = slice(first * queries, last * queries)
        dk = dot(ds_ref[:, span], stacked(q_ref, first, last), NN) * softmax_scale
        dv = dot(w_ref[:, span], stacked(do_ref, first, last), NN)
        for part, grad in ((0, dk), (1, dv)):
            for r in range(rows):
                at_lane = pl.ds((2 * r + part) * features + group * HEAD_SIZE, HEAD_SIZE)
                keep_ref[:, at_lane] = grad[r * slots:r * slots + half]
                send_ref[:, at_lane] = grad[r * slots + half:(r + 1) * slots].astype(bf16)


def back_kernel(
    group, place, rows, per_group, per, aliased, q_ref, do_ref, kv_ref, shared_ref, ws_ref, dss_ref, joined_ref,
    e_ref, dp_ref, *refs,
):
    out_ref, dq_ref, dkv_ref, w_ref, ds_ref = refs[aliased:]
    queries = q_ref.shape[0]
    features = kv_ref.shape[2]
    lanes = slice(group * HEAD_SIZE, (group + 1) * HEAD_SIZE)

    def turned(part):
        shared = shared_rows_of(shared_ref, rows, features, part, group)
        return jnp.concatenate([shared, kv_ref[part, :, lanes]], axis=0).T

    keys_t, values_t = turned(0), turned(1)

    def unstack(ref, lo, value):
        back = value.T
        for h in range(per):
            ref[:, (lo + h) * HEAD_SIZE:(lo + h + 1) * HEAD_SIZE] = back[h * queries:(h + 1) * queries]

    for lo in range(0, per_group, per):
        span = slice(lo * queries, (lo + per) * queries)
        stored = slice((place + lo) * queries, (place + lo + per) * queries)
        whole = slice((group * per_group + lo) * queries, (group * per_group + lo + per) * queries)
        p = e_ref[:, stored] * joined_ref[0:1, whole]
        w = p.astype(bf16)
        ds = (p * (dp_ref[:, stored] - joined_ref[1:2, whole])).astype(bf16)
        w_ref[:, span] = w
        ds_ref[:, span] = ds
        o_t = dot(values_t, jnp.concatenate([ws_ref[:, whole], w], axis=0), NN)
        unstack(out_ref, lo, o_t.astype(bf16))
        dq_t = dot(keys_t, jnp.concatenate([dss_ref[:, whole], ds], axis=0), NN) * softmax_scale
        unstack(dq_ref, lo, dq_t.astype(bf16))
    first, last = group * per_group, (group + 1) * per_group
    dk = dot(ds_ref[...], stacked(q_ref, first, last), NN) * softmax_scale
    dv = dot(w_ref[...], stacked(do_ref, first, last), NN)
    dkv_ref[0] = dk.astype(bf16)
    dkv_ref[1] = dv.astype(bf16)


def pack_kernel(trunk_rows, features, trunk_ref, turn_ref, out_ref):
    rows = out_ref.shape[1] // (2 * features)
    for r in range(rows):
        for part in range(2):
            lane = (2 * r + part) * features
            if r < trunk_rows:
                piece = trunk_ref[part, r:r + 1, :]
            else:
                piece = turn_ref[part, r - trunk_rows:r - trunk_rows + 1, :]
            out_ref[:, lane:lane + features] = piece


def finish_kernel(trunk_rows, features, total_ref, last_ref, trunk_ref, turn_ref):
    total = (total_ref[...] + last_ref[...].astype(f32)).astype(bf16)
    rows = total.shape[1] // (2 * features)
    for r in range(rows):
        for part in range(2):
            lane = (2 * r + part) * features
            piece = total[:, lane:lane + features]
            if r < trunk_rows:
                trunk_ref[part, r:r + 1, :] = piece
            else:
                turn_ref[part, r - trunk_rows:r - trunk_rows + 1, :] = piece


params = pltpu.CompilerParams(vmem_limit_bytes=16 * 2 ** 20)


def on_device(mesh, query, branch_kv, turn_kv, trunk_kv, grad_out, lengths, parents):
    steps = exchange_steps(mesh)
    slots = 2 ** len(steps)
    queries, width = query.shape
    features = branch_kv.shape[2]
    groups = features // HEAD_SIZE
    per_group = width // features
    per = 2 if per_group % 2 == 0 else 1
    parts = groups
    trunk_rows, turn_rows = trunk_kv.shape[1], turn_kv.shape[1]
    rows = trunk_rows + turn_rows
    flat = rows * 2 * features
    spread = queries * per_group
    shape = jax.ShapeDtypeStruct

    own_parts = []
    for part in range(parts):
        own_parts.append(pl.pallas_call(
            functools.partial(own_kernel, part * groups // parts, per_group, per),
            in_specs=[smem, vmem, vmem, vmem],
            out_specs=[vmem] * 3,
            out_shape=[
                shape((queries, spread * groups // parts), f32),
                shape((queries, spread * groups // parts), f32),
                shape((8, spread * groups // parts), f32),
            ],
            compiler_params=params,
        )(lengths, query, grad_out, branch_kv))

    near = pl.pallas_call(
        functools.partial(pack_kernel, trunk_rows, features),
        in_specs=[vmem] * 2,
        out_specs=vmem,
        out_shape=shape((1, flat), bf16),
        compiler_params=params,
        name="pack",
    )(trunk_kv, turn_kv)
    for k, step in enumerate(steps):
        if k:
            near = jnp.concatenate([near, far], axis=0)
        far = swap(near, step)

    held, shared_w, shared_ds, joined, total, send = pl.pallas_call(
        functools.partial(
            shared_kernel, steps, trunk_rows, turn_rows, mesh.shape["turn"], per_group, per, parts
        ),
        in_specs=[smem] + [vmem] * (4 + parts),
        out_specs=[vmem] * 6,
        out_shape=[
            shape((slots, flat), bf16),
            shape((slots * rows, spread * groups), bf16),
            shape((slots * rows, spread * groups), bf16),
            shape((8, spread * groups), f32),
            shape((slots // 2, flat), f32),
            shape((slots // 2, flat), bf16),
        ],
        compiler_params=params,
        name="shared",
    )(parents, near, far, query, grad_out, *[p[2] for p in own_parts])

    made = ()
    block = lambda g: pl.BlockSpec((queries, spread_width), lambda i: (0, g))
    spread_width = width // groups
    for group in range(groups):
        part, place = divmod(group, groups // parts)
        e, dp, _ = own_parts[part]
        made = pl.pallas_call(
            functools.partial(back_kernel, group, place * per_group, rows, per_group, per, len(made)),
            grid=(1,),
            in_specs=[vmem] * 9 + [pl.BlockSpec(memory_space=pl.ANY)] * len(made),
            out_specs=[
                block(group), block(group),
                pl.BlockSpec((2, queries, HEAD_SIZE), lambda i, g=group: (0, 0, g)),
            ],
            out_shape=[
                shape(query.shape, bf16), shape(query.shape, bf16), shape(branch_kv.shape, bf16)
            ],
            scratch_shapes=[pltpu.VMEM((queries, spread), bf16)] * 2,
            input_output_aliases={9 + i: i for i in range(len(made))},
            compiler_params=params,
        )(query, grad_out, branch_kv, held, shared_w, shared_ds, joined, e, dp, *made)

    for k in reversed(range(len(steps))):
        came = swap(send, steps[k])
        if k:
            total = total + came.astype(f32)
            half = total.shape[0] // 2
            send, total = total[half:].astype(bf16), total[:half]
    grad_trunk, grad_turn = pl.pallas_call(
        functools.partial(finish_kernel, trunk_rows, features),
        in_specs=[vmem] * 2,
        out_shape=[shape(trunk_kv.shape, bf16), shape(turn_kv.shape, bf16)],
        compiler_params=params,
        name="finish",
    )(total, came)
    return (*made, grad_turn, grad_trunk)


def solution(mesh):
    everywhere = ("parts", "turn", "branch")
    by_row = P(everywhere, None)
    by_middle = P(None, everywhere, None)

    def layer(*args):
        return on_device(mesh, *args)

    return jax.shard_map(
        layer,
        mesh=mesh,
        in_specs=(by_row, by_middle, by_middle, by_middle, by_row, by_row, P("parts")),
        out_specs=(by_row, by_row, by_middle, by_middle, by_middle),
        check_vma=False,
    )
```

time: 42.4 us -> 43.9 us (1.035)
  waiting for transfers between devices: 13.4 us -> 10.1 us
  Pallas kernels: 8.46 us -> 11.4 us
  local copies, waits for them, and re-layouts: 3.27 us -> 5.54 us
  other arithmetic: 1.14 us -> 0.18 us
    unnamed x4 -> x20, local copies, waits for them, and re-layouts: 1.29 us -> 5.48 us
    ppermute x8, waiting for transfers between devices: 13.4 us -> 10.1 us  [swap(): return lax.ppermute(x, axis, [(i, i ^ bit) for i in range(size)])]
    pallas_call x1 -> x11, Pallas kernels: 8.46 us -> 11.4 us  [the longest x4 5.04 us: on_device(): pl.pallas_call(functools.partial(back_kernel, group, place * per_group, r...]
    concatenate x1 -> x0, local copies, waits for them, and re-layouts: 1.3 us -> none  [on_device(): held = jnp.concatenate([held, swap(held, axis, bit, size)], axis=0)]
    add x3, other arithmetic: 0.93 us -> 0.04 us  [on_device(): total = total + came.astype(f32)]
    slice x2 -> x0, local copies, waits for them, and re-layouts: 0.59 us -> none  [the longest x1 0.58 us: on_device(): total[:, :trunk_rows]]
  transfers between devices with their start and end apart: 8 -> 8, of which waited for: 8 -> 6; matrix products, arithmetic and copies ran while one was open for 0% -> 0% of each run, Pallas kernels for 0% -> 20%
where the time goes in v2:
time: 43.9 us; the launch traced here: 43.6 us
  starting transfers between devices  15.5 us (35%)
  Pallas kernels  11.4 us (26%)
  waiting for transfers between devices  10.1 us (23%)
  local copies, waits for them, and re-layouts  5.54 us (13%)
  between operations  0.8 us (2%)
    ppermute x8, starting transfers between devices, swap(): return lax.ppermute(x, axis, [(i, i ^ bit) for i in range(size)])  15.5 us
    ppermute x8, waiting for transfers between devices, swap(): return lax.ppermute(x, axis, [(i, i ^ bit) for i in range(size)])  10.1 us
    unnamed x20, local copies, waits for them, and re-layouts  5.48 us
    pallas_call x4, Pallas kernels, on_device(): pl.pallas_call(functools.partial(back_kernel, group, place * per_group, r...  5.04 us
    pallas_call x4, Pallas kernels, on_device(): pl.pallas_call(functools.partial(own_kernel, part * groups // parts, per_...  3.64 us
    pallas_call x1, Pallas kernels, on_device(): pl.pallas_call(functools.partial(shared_kernel, steps, trunk_rows, turn_r...  2.13 us
  transfers between devices with their start and end apart: 8, of which 6 were waited for; matrix products, arithmetic and copies ran while one was open for 0% of the time, Pallas kernels for 20%

profile of v2, /device:TPU:0, one launch (start us, length us, event | category | flops | bytes accessed | tf_op | source)
XLA Modules:
  0.0 43.6 jit_solution(12751441194617630961)
XLA Ops:
  0.6 0.0 copy-start.7
  0.6 0.7 %copy.21.trunk_ref = bf16[2,1,512]{2,1,0:T(2,128)(2,1)S(1)} copy(bf16[2,1,512]{2,0,1:T(2,128)(2,1)} %param.10) | data formatting | bytes 4096 | tf_op args[3]
  1.3 0.0 copy-done.7
  1.3 4.1 %collective-permute-start = (bf16[1,3072]{1,0:T(2,128)(2,1)S(1)}, bf16[1,3072]{1,0:T(2,128)(2,1)S(1)}, u32[]{:S(2)}, u32[]{:S(2)}) collective-permute-start(bf16[1,3072]{1,0:T(2,128)(2,1)S(1)} %pack.1), channel_id=1, source_target_pairs={{0,2},{1,3},{2,0},{3,1},{4,6},{5,7},{6,4},{7,5},{8,10},{9,11},{10,... | collective-permute-start | bytes 18440 | tf_op jit(solution)/shard_map/ppermute | solution.py:38
  5.5 1.7 %collective-permute-done = bf16[1,3072]{1,0:T(2,128)(2,1)S(1)} collective-permute-done((bf16[1,3072]{1,0:T(2,128)(2,1)S(1)}, bf16[1,3072]{1,0:T(2,128)(2,1)S(1)}, u32[]{:S(2)}, u32[]{:S(2)}) %collective-permute-start) | collective-permute-done | bytes 6176 | tf_op jit(solution)/shard_map/ppermute | solution.py:38
  7.2 2.0 %collective-permute-start.1 = (bf16[2,3072]{1,0:T(2,128)(2,1)S(1)}, bf16[2,3072]{1,0:T(2,128)(2,1)S(1)}, u32[]{:S(2)}, u32[]{:S(2)}) collective-permute-start(bf16[2,3072]{1,0:T(2,128)(2,1)S(1)} %pad_maximum_fusion.2), channel_id=1, source_target_pairs={{0,1},{1,0},{2,3},{3,2},{4,5},{5,4},{6,7},{7,6},{8,9},{9,8},{10,11... | collective-permute-start | bytes 36872 | tf_op jit(solution)/shard_map/ppermute | solution.py:38
  9.2 1.8 %collective-permute-done.1 = bf16[2,3072]{1,0:T(2,128)(2,1)S(1)} collective-permute-done((bf16[2,3072]{1,0:T(2,128)(2,1)S(1)}, bf16[2,3072]{1,0:T(2,128)(2,1)S(1)}, u32[]{:S(2)}, u32[]{:S(2)}) %collective-permute-start.1) | collective-permute-done | bytes 12320 | tf_op jit(solution)/shard_map/ppermute | solution.py:38
  11.0 0.0 copy-start.6
  11.0 1.9 %collective-permute-start.2 = (bf16[4,3072]{1,0:T(4,128)(2,1)S(1)}, bf16[4,3072]{1,0:T(4,128)(2,1)S(1)}, u32[]{:S(2)}, u32[]{:S(2)}) collective-permute-start(bf16[4,3072]{1,0:T(4,128)(2,1)S(1)} %pad_maximum_fusion.1), channel_id=1, source_target_pairs={{0,8},{4,12},{8,0},{12,4},{1,9},{5,13},{9,1},{13,5},{2,10},{6,14},... | collective-permute-start | bytes 73736 | tf_op jit(solution)/shard_map/ppermute | solution.py:38
  12.9 2.0 %collective-permute-done.2 = bf16[4,3072]{1,0:T(4,128)(2,1)S(1)} collective-permute-done((bf16[4,3072]{1,0:T(4,128)(2,1)S(1)}, bf16[4,3072]{1,0:T(4,128)(2,1)S(1)}, u32[]{:S(2)}, u32[]{:S(2)}) %collective-permute-start.2) | collective-permute-done | bytes 24608 | tf_op jit(solution)/shard_map/ppermute | solution.py:38
  14.9 0.1 pad_maximum_fusion.near_ref
  15.0 0.1 collective-permute-start.3
  15.0 0.0 copy-done.6
  15.1 0.0 copy-start
  15.1 1.2 %copy-done = bf16[128,4096]{1,0:T(8,128)(2,1)S(1)} copy-done((bf16[128,4096]{1,0:T(8,128)(2,1)S(1)}, bf16[128,4096]{1,0:T(8,128)(2,1)}, u32[]{:S(2)}) %copy-start) | copy-done | bytes 1048600
  16.3 0.0 copy-start.2
  16.3 1.2 %copy-done.2 = bf16[128,4096]{1,0:T(8,128)(2,1)S(1)} copy-done((bf16[128,4096]{1,0:T(8,128)(2,1)S(1)}, bf16[128,4096]{1,0:T(8,128)(2,1)}, u32[]{:S(2)}) %copy-start.2) | copy-done | bytes 1048600
  17.5 0.0 copy-start.4
  17.5 0.9 %copy-done.4 = bf16[2,128,512]{2,1,0:T(8,128)(2,1)S(1)} copy-done((bf16[2,128,512]{2,1,0:T(8,128)(2,1)S(1)}, bf16[2,128,512]{2,1,0:T(8,128)(2,1)}, u32[]{:S(2)}) %copy-start.4) | copy-done | bytes 262168
  18.5 0.9 %shard_map.111 = (f32[128,1024]{1,0:T(8,128)S(1)}, f32[128,1024]{1,0:T(8,128)S(1)}, f32[8,1024]{1,0:T(8,128)S(1)}) custom-call(s32[1,4]{1,0:T(1,128)S(1)} %copy-done.6, bf16[128,4096]{1,0:T(8,128)(2,1)S(1)} %copy-done, bf16[128,4096]{1,0:T(8,128)(2,1)S(1)} %copy-done.2, bf16[2,128,512]{2,1,0:T(8,128)(2,1)S(1)} %copy-done.4), custom_call_target="tpu_custom_call" | custom-call | tf_op jit(solution)/shard_map/pallas_call | solution.py:246
  19.4 0.9 %shard_map.110 = (f32[128,1024]{1,0:T(8,128)S(1)}, f32[128,1024]{1,0:T(8,128)S(1)}, f32[8,1024]{1,0:T(8,128)S(1)}) custom-call(s32[1,4]{1,0:T(1,128)S(1)} %copy-done.6, bf16[128,4096]{1,0:T(8,128)(2,1)S(1)} %copy-done, bf16[128,4096]{1,0:T(8,128)(2,1)S(1)} %copy-done.2, bf16[2,128,512]{2,1,0:T(8,128)(2,1)S(1)} %copy-done.4), custom_call_target="tpu_custom_call" | custom-call | tf_op jit(solution)/shard_map/pallas_call | solution.py:246
  20.3 0.9 %shard_map.113 = (f32[128,1024]{1,0:T(8,128)S(1)}, f32[128,1024]{1,0:T(8,128)S(1)}, f32[8,1024]{1,0:T(8,128)S(1)}) custom-call(s32[1,4]{1,0:T(1,128)S(1)} %copy-done.6, bf16[128,4096]{1,0:T(8,128)(2,1)S(1)} %copy-done, bf16[128,4096]{1,0:T(8,128)(2,1)S(1)} %copy-done.2, bf16[2,128,512]{2,1,0:T(8,128)(2,1)S(1)} %copy-done.4), custom_call_target="tpu_custom_call" | custom-call | tf_op jit(solution)/shard_map/pallas_call | solution.py:246
  21.2 0.0 copy-start.1
  21.2 0.0 copy-start.3
  21.2 0.9 %shard_map.112 = (f32[128,1024]{1,0:T(8,128)S(1)}, f32[128,1024]{1,0:T(8,128)S(1)}, f32[8,1024]{1,0:T(8,128)S(1)}) custom-call(s32[1,4]{1,0:T(1,128)S(1)} %copy-done.6, bf16[128,4096]{1,0:T(8,128)(2,1)S(1)} %copy-done, bf16[128,4096]{1,0:T(8,128)(2,1)S(1)} %copy-done.2, bf16[2,128,512]{2,1,0:T(8,128)(2,1)S(1)} %copy-done.4), custom_call_target="tpu_custom_call" | custom-call | tf_op jit(solution)/shard_map/pallas_call | solution.py:246
  22.2 0.0 collective-permute-done.3.far_ref
  22.2 0.0 copy-start.8
  22.2 0.3 copy-done.1
  22.4 0.3 copy-done.3
  22.8 0.2 copy-done.8
  23.0 2.1 %shared.1 = (bf16[16,3072]{1,0:T(8,128)(2,1)S(1)}, bf16[48,4096]{1,0:T(8,128)(2,1)S(1)}, bf16[48,4096]{1,0:T(8,128)(2,1)S(1)}, f32[8,4096]{1,0:T(8,128)S(1)}, f3...) custom-call(s32[4]{0:T(128)S(1)} %copy-done.8, bf16[8,3072]{1,0:T(8,128)(2,1)S(1)} %pad_maximum_fusion.near_ref, ...), custom_call_target="tpu_custom_call" | custom-call | tf_op jit(solution)/shard_map/shared/pallas_call | solution.py:271
  25.1 0.6 %collective-permute-start.4 = (bf16[8,3072]{1,0:T(8,128)(2,1)S(1)}, bf16[8,3072]{1,0:T(8,128)(2,1)S(1)}, u32[]{:S(2)}, u32[]{:S(2)}) collective-permute-start(bf16[8,3072]{1,0:T(8,128)(2,1)S(1)} %get-tuple-element.66), channel_id=1, source_target_pairs={{0,4},{4,0},{8,12},{12,8},{1,5},{5,1},{9,13},{13,9},{2,6},{6,2},{1... | collective-permute-start | bytes 147464 | tf_op jit(solution)/shard_map/ppermute | solution.py:38
  25.7 0.9 %collective-permute-done.4 = bf16[8,3072]{1,0:T(8,128)(2,1)S(1)} collective-permute-done((bf16[8,3072]{1,0:T(8,128)(2,1)S(1)}, bf16[8,3072]{1,0:T(8,128)(2,1)S(1)}, u32[]{:S(2)}, u32[]{:S(2)}) %collective-permute-start.4) | collective-permute-done | bytes 49184 | tf_op jit(solution)/shard_map/ppermute | solution.py:38
  26.5 0.0 copy-start.5
  26.6 1.9 %collective-permute-start.5 = (bf16[4,3072]{1,0:T(4,128)(2,1)S(1)}, bf16[4,3072]{1,0:T(4,128)(2,1)S(1)}, u32[]{:S(2)}, u32[]{:S(2)}) collective-permute-start(bf16[4,3072]{1,0:T(4,128)(2,1)S(1)} %slice.38), channel_id=1, source_target_pairs={{0,8},{4,12},{8,0},{12,4},{1,9},{5,13},{9,1},{13,5},{2,10},{6,14},... | collective-permute-start | bytes 73736 | tf_op jit(solution)/shard_map/ppermute | solution.py:38
  28.5 2.0 %collective-permute-done.5 = bf16[4,3072]{1,0:T(4,128)(2,1)S(1)} collective-permute-done((bf16[4,3072]{1,0:T(4,128)(2,1)S(1)}, bf16[4,3072]{1,0:T(4,128)(2,1)S(1)}, u32[]{:S(2)}, u32[]{:S(2)}) %collective-permute-start.5) | collective-permute-done | bytes 24608 | tf_op jit(solution)/shard_map/ppermute | solution.py:38
  30.5 2.0 %collective-permute-start.6 = (bf16[2,3072]{1,0:T(2,128)(2,1)S(1)}, bf16[2,3072]{1,0:T(2,128)(2,1)S(1)}, u32[]{:S(2)}, u32[]{:S(2)}) collective-permute-start(bf16[2,3072]{1,0:T(2,128)(2,1)S(1)} %slice.39), channel_id=1, source_target_pairs={{0,1},{1,0},{2,3},{3,2},{4,5},{5,4},{6,7},{7,6},{8,9},{9,8},{10,11... | collective-permute-start | bytes 36872 | tf_op jit(solution)/shard_map/ppermute | solution.py:38
  32.5 1.8 %collective-permute-done.6 = bf16[2,3072]{1,0:T(2,128)(2,1)S(1)} collective-permute-done((bf16[2,3072]{1,0:T(2,128)(2,1)S(1)}, bf16[2,3072]{1,0:T(2,128)(2,1)S(1)}, u32[]{:S(2)}, u32[]{:S(2)}) %collective-permute-start.6) | collective-permute-done | bytes 12320 | tf_op jit(solution)/shard_map/ppermute | solution.py:38
  34.3 3.0 %collective-permute-start.7 = (bf16[1,3072]{1,0:T(2,128)(2,1)S(1)}, bf16[1,3072]{1,0:T(2,128)(2,1)S(1)}, u32[]{:S(2)}, u32[]{:S(2)}) collective-permute-start(bf16[1,3072]{1,0:T(2,128)(2,1)S(1)} %slice.40), channel_id=1, source_target_pairs={{0,2},{1,3},{2,0},{3,1},{4,6},{5,7},{6,4},{7,5},{8,10},{9,11},{10,... | collective-permute-start | bytes 18440 | tf_op jit(solution)/shard_map/ppermute | solution.py:38
  37.3 0.0 copy-done.5
  37.3 1.3 %shard_map.114 = (bf16[128,4096]{1,0:T(8,128)(2,1)}, bf16[128,4096]{1,0:T(8,128)(2,1)}, bf16[2,128,512]{2,1,0:T(8,128)(2,1)}) custom-call(bf16[128,4096]{1,0:T(8,128)(2,1)S(1)} %copy-done.1, bf16[128,4096]{1,0:T(8,128)(2,1)S(1)} %copy-done.3, bf16[2,128,512]{2,1,0:T(8,128)(2,1)S(1)} %copy-done.5, bf16[16,3072]{1,0:T(8,128)(2,1)S(1)} %get-tuple-element.41.shared_ref, ...), custom_call_target="tpu_custom_call" | custom-call | tf_op jit(solution)/shard_map/pallas_call | solution.py:295
  38.6 1.2 %shard_map.115 = (bf16[128,4096]{1,0:T(8,128)(2,1)}, bf16[128,4096]{1,0:T(8,128)(2,1)}, bf16[2,128,512]{2,1,0:T(8,128)(2,1)}) custom-call(bf16[128,4096]{1,0:T(8,128)(2,1)S(1)} %copy-done.1, bf16[128,4096]{1,0:T(8,128)(2,1)S(1)} %copy-done.3, bf16[2,128,512]{2,1,0:T(8,128)(2,1)S(1)} %copy-done.5, ...), custom_call_target="tpu_custom_call", output_to_operand_aliasing={{0}: (9, {}), {1}: (10, {}), {2}: (11, {})} | custom-call | tf_op jit(solution)/shard_map/pallas_call | solution.py:295
  39.8 1.3 %shard_map.116 = (bf16[128,4096]{1,0:T(8,128)(2,1)}, bf16[128,4096]{1,0:T(8,128)(2,1)}, bf16[2,128,512]{2,1,0:T(8,128)(2,1)}) custom-call(bf16[128,4096]{1,0:T(8,128)(2,1)S(1)} %copy-done.1, bf16[128,4096]{1,0:T(8,128)(2,1)S(1)} %copy-done.3, bf16[2,128,512]{2,1,0:T(8,128)(2,1)S(1)} %copy-done.5, ...), custom_call_target="tpu_custom_call", output_to_operand_aliasing={{0}: (9, {}), {1}: (10, {}), {2}: (11, {})} | custom-call | tf_op jit(solution)/shard_map/pallas_call | solution.py:295
  41.1 1.3 %shard_map.117 = (bf16[128,4096]{1,0:T(8,128)(2,1)}, bf16[128,4096]{1,0:T(8,128)(2,1)}, bf16[2,128,512]{2,1,0:T(8,128)(2,1)}) custom-call(bf16[128,4096]{1,0:T(8,128)(2,1)S(1)} %copy-done.1, bf16[128,4096]{1,0:T(8,128)(2,1)S(1)} %copy-done.3, bf16[2,128,512]{2,1,0:T(8,128)(2,1)S(1)} %copy-done.5, ...), custom_call_target="tpu_custom_call", output_to_operand_aliasing={{0}: (9, {}), {1}: (10, {}), {2}: (11, {})} | custom-call | tf_op jit(solution)/shard_map/pallas_call | solution.py:295
  42.4 0.0 collective-permute-done.7.last_ref
  42.4 0.6 %finish.1 = (bf16[2,1,512]{2,1,0:T(2,128)(2,1)S(1)}, bf16[2,2,512]{2,1,0:T(2,128)(2,1)}) custom-call(f32[1,3072]{1,0:T(1,128)S(1)} %slice.31.total_ref, bf16[1,3072]{1,0:T(2,128)(2,1)S(1)} %collective-permute-done.7.last_ref), custom_call_target="tpu_custom_call" | custom-call | tf_op jit(solution)/shard_map/finish/pallas_call | solution.py:317
  43.0 0.6 %copy.22 = bf16[2,1,512]{2,0,1:T(2,128)(2,1)} copy(bf16[2,1,512]{2,1,0:T(2,128)(2,1)S(1)} %get-tuple-element.73) | data formatting | bytes 4096
  (10 shorter events, 0.2 us)
Async XLA Ops:
  0.6 0.7 %copy-start.7 = (bf16[2,2,512]{2,1,0:T(2,128)(2,1)S(1)}, bf16[2,2,512]{2,1,0:T(2,128)(2,1)}, u32[]{:S(2)}) copy-start(bf16[2,2,512]{2,1,0:T(2,128)(2,1)} %turn_ref.1) | copy-start | bytes 12292
  1.3 5.8 %collective-permute-start = (bf16[1,3072]{1,0:T(2,128)(2,1)S(1)}, bf16[1,3072]{1,0:T(2,128)(2,1)S(1)}, u32[]{:S(2)}, u32[]{:S(2)}) collective-permute-start(bf16[1,3072]{1,0:T(2,128)(2,1)S(1)} %pack.1), channel_id=1, source_target_pairs={{0,2},{1,3},{2,0},{3,1},{4,6},{5,7},{6,4},{7,5},{8,10},{9,11},{10,... | collective-permute-start | bytes 18440 | tf_op jit(solution)/shard_map/ppermute | solution.py:38
  7.2 3.8 %collective-permute-start.1 = (bf16[2,3072]{1,0:T(2,128)(2,1)S(1)}, bf16[2,3072]{1,0:T(2,128)(2,1)S(1)}, u32[]{:S(2)}, u32[]{:S(2)}) collective-permute-start(bf16[2,3072]{1,0:T(2,128)(2,1)S(1)} %pad_maximum_fusion.2), channel_id=1, source_target_pairs={{0,1},{1,0},{2,3},{3,2},{4,5},{5,4},{6,7},{7,6},{8,9},{9,8},{10,11... | collective-permute-start | bytes 36872 | tf_op jit(solution)/shard_map/ppermute | solution.py:38
  11.0 4.1 %copy-start.6 = (s32[1,4]{1,0:T(1,128)S(1)}, s32[1,4]{1,0:T(1,128)}, u32[]{:S(2)}) copy-start(s32[1,4]{1,0:T(1,128)} %lengths_ref.7) | copy-start | bytes 52
  11.0 3.9 %collective-permute-start.2 = (bf16[4,3072]{1,0:T(4,128)(2,1)S(1)}, bf16[4,3072]{1,0:T(4,128)(2,1)S(1)}, u32[]{:S(2)}, u32[]{:S(2)}) collective-permute-start(bf16[4,3072]{1,0:T(4,128)(2,1)S(1)} %pad_maximum_fusion.1), channel_id=1, source_target_pairs={{0,8},{4,12},{8,0},{12,4},{1,9},{5,13},{9,1},{13,5},{2,10},{6,14},... | collective-permute-start | bytes 73736 | tf_op jit(solution)/shard_map/ppermute | solution.py:38
  15.0 7.2 %collective-permute-start.3 = (bf16[8,3072]{1,0:T(8,128)(2,1)S(1)}, bf16[8,3072]{1,0:T(8,128)(2,1)S(1)}, u32[]{:S(2)}, u32[]{:S(2)}) collective-permute-start(bf16[8,3072]{1,0:T(8,128)(2,1)S(1)} %pad_maximum_fusion.near_ref), channel_id=1, source_target_pairs={{0,4},{4,0},{8,12},{12,8},{1,5},{5,1},{9,13},{13,9},{2,6},{6,2},{1... | collective-permute-start | bytes 147464 | tf_op jit(solution)/shard_map/ppermute | solution.py:38
  15.1 1.2 %copy-start = (bf16[128,4096]{1,0:T(8,128)(2,1)S(1)}, bf16[128,4096]{1,0:T(8,128)(2,1)}, u32[]{:S(2)}) copy-start(bf16[128,4096]{1,0:T(8,128)(2,1)} %q_ref.17) | copy-start | bytes 3145732
  16.3 1.2 %copy-start.2 = (bf16[128,4096]{1,0:T(8,128)(2,1)S(1)}, bf16[128,4096]{1,0:T(8,128)(2,1)}, u32[]{:S(2)}) copy-start(bf16[128,4096]{1,0:T(8,128)(2,1)} %do_ref.17) | copy-start | bytes 3145732
  17.5 0.9 %copy-start.4 = (bf16[2,128,512]{2,1,0:T(8,128)(2,1)S(1)}, bf16[2,128,512]{2,1,0:T(8,128)(2,1)}, u32[]{:S(2)}) copy-start(bf16[2,128,512]{2,1,0:T(8,128)(2,1)} %kv_ref.15) | copy-start | bytes 786436
  21.2 1.2 %copy-start.1 = (bf16[128,4096]{1,0:T(8,128)(2,1)S(1)}, bf16[128,4096]{1,0:T(8,128)(2,1)}, u32[]{:S(2)}) copy-start(bf16[128,4096]{1,0:T(8,128)(2,1)} %q_ref.17) | copy-start | bytes 3145732
  21.2 1.5 %copy-start.3 = (bf16[128,4096]{1,0:T(8,128)(2,1)S(1)}, bf16[128,4096]{1,0:T(8,128)(2,1)}, u32[]{:S(2)}) copy-start(bf16[128,4096]{1,0:T(8,128)(2,1)} %do_ref.17) | copy-start | bytes 3145732
  22.2 0.8 %copy-start.8 = (s32[4]{0:T(128)S(1)}, s32[4]{0:T(128)}, u32[]{:S(2)}) copy-start(s32[4]{0:T(128)} %parents_ref.1) | copy-start | bytes 52
  25.1 1.4 %collective-permute-start.4 = (bf16[8,3072]{1,0:T(8,128)(2,1)S(1)}, bf16[8,3072]{1,0:T(8,128)(2,1)S(1)}, u32[]{:S(2)}, u32[]{:S(2)}) collective-permute-start(bf16[8,3072]{1,0:T(8,128)(2,1)S(1)} %get-tuple-element.66), channel_id=1, source_target_pairs={{0,4},{4,0},{8,12},{12,8},{1,5},{5,1},{9,13},{13,9},{2,6},{6,2},{1... | collective-permute-start | bytes 147464 | tf_op jit(solution)/shard_map/ppermute | solution.py:38
  26.5 10.8 %copy-start.5 = (bf16[2,128,512]{2,1,0:T(8,128)(2,1)S(1)}, bf16[2,128,512]{2,1,0:T(8,128)(2,1)}, u32[]{:S(2)}) copy-start(bf16[2,128,512]{2,1,0:T(8,128)(2,1)} %kv_ref.15) | copy-start | bytes 786436
  26.6 3.9 %collective-permute-start.5 = (bf16[4,3072]{1,0:T(4,128)(2,1)S(1)}, bf16[4,3072]{1,0:T(4,128)(2,1)S(1)}, u32[]{:S(2)}, u32[]{:S(2)}) collective-permute-start(bf16[4,3072]{1,0:T(4,128)(2,1)S(1)} %slice.38), channel_id=1, source_target_pairs={{0,8},{4,12},{8,0},{12,4},{1,9},{5,13},{9,1},{13,5},{2,10},{6,14},... | collective-permute-start | bytes 73736 | tf_op jit(solution)/shard_map/ppermute | solution.py:38
  30.5 3.8 %collective-permute-start.6 = (bf16[2,3072]{1,0:T(2,128)(2,1)S(1)}, bf16[2,3072]{1,0:T(2,128)(2,1)S(1)}, u32[]{:S(2)}, u32[]{:S(2)}) collective-permute-start(bf16[2,3072]{1,0:T(2,128)(2,1)S(1)} %slice.39), channel_id=1, source_target_pairs={{0,1},{1,0},{2,3},{3,2},{4,5},{5,4},{6,7},{7,6},{8,9},{9,8},{10,11... | collective-permute-start | bytes 36872 | tf_op jit(solution)/shard_map/ppermute | solution.py:38
  34.3 8.0 %collective-permute-start.7 = (bf16[1,3072]{1,0:T(2,128)(2,1)S(1)}, bf16[1,3072]{1,0:T(2,128)(2,1)S(1)}, u32[]{:S(2)}, u32[]{:S(2)}) collective-permute-start(bf16[1,3072]{1,0:T(2,128)(2,1)S(1)} %slice.40), channel_id=1, source_target_pairs={{0,2},{1,3},{2,0},{3,1},{4,6},{5,7},{6,4},{7,5},{8,10},{9,11},{10,... | collective-permute-start | bytes 18440 | tf_op jit(solution)/shard_map/ppermute | solution.py:38

commit v3 on v2

v3 whole, which is shorter than its diff:
```python
import functools
import math

import jax
import jax.numpy as jnp
from jax import lax
from jax.experimental import pallas as pl
from jax.experimental.pallas import tpu as pltpu
from jax.sharding import PartitionSpec as P


HEAD_SIZE = 128
masked_score = -1e30
softmax_scale = 1.0 / math.sqrt(HEAD_SIZE)
exp2_scale = softmax_scale * math.log2(math.e)
f32 = jnp.float32
bf16 = jnp.bfloat16
NT = (((1,), (1,)), ((), ()))
NN = (((1,), (0,)), ((), ()))
vmem = pl.BlockSpec(memory_space=pltpu.VMEM)
hbm = pl.BlockSpec(memory_space=pltpu.HBM)


def exchange_steps(mesh):
    steps = []
    for axis in ("branch", "turn"):
        size = mesh.shape[axis]
        assert size & (size - 1) == 0
        bit = size // 2
        while bit:
            steps.append((axis, bit, size))
            bit //= 2
    return steps


def swap(x, step):
    axis, bit, size = step
    return lax.ppermute(x, axis, [(i, i ^ bit) for i in range(size)])


def in_hbm(x):
    return pltpu.with_memory_space_constraint(x, pltpu.HBM)


def dot(a, b, dims):
    return lax.dot_general(a, b, dims, preferred_element_type=f32)


def load_kernel(
    steps, trunk_rows, turn_rows, turns, q_hbm, do_hbm, kv_hbm, lengths_hbm, parents_hbm,
    q_ref, do_ref, kv_ref, own_bias_ref, bias_ref, lengths_ref, parents_ref, sems,
):
    queries = q_hbm.shape[0]
    slots = 2 ** len(steps)
    small = [
        pltpu.make_async_copy(lengths_hbm, lengths_ref, sems.at[0]),
        pltpu.make_async_copy(parents_hbm, parents_ref, sems.at[1]),
    ]
    for copy in small:
        copy.start()
    for part in range(2):
        for g in range(kv_hbm.shape[2] // HEAD_SIZE):
            pltpu.make_async_copy(
                kv_hbm.at[part, :, pl.ds(g * HEAD_SIZE, HEAD_SIZE)], kv_ref.at[part, g], sems.at[2]
            ).start()
    for h in range(q_hbm.shape[1] // HEAD_SIZE):
        lanes = pl.ds(h * HEAD_SIZE, HEAD_SIZE)
        place = pl.ds(h * queries, queries)
        pltpu.make_async_copy(q_hbm.at[:, lanes], q_ref.at[place], sems.at[3]).start()
        pltpu.make_async_copy(do_hbm.at[:, lanes], do_ref.at[place], sems.at[4]).start()
    for copy in small:
        copy.wait()

    key_at = lax.broadcasted_iota(jnp.int32, (queries, queries), 0)
    query_at = lax.broadcasted_iota(jnp.int32, (queries, queries), 1)
    start = jnp.zeros_like(query_at)
    end = jnp.int32(0)
    for c in range(lengths_ref.shape[1]):
        end = end + lengths_ref[0, c]
        start = jnp.where(query_at >= end, end, start)
    inside = (key_at >= start) & (key_at <= query_at)
    own_bias_ref[...] = jnp.where(inside, 0.0, masked_score).astype(f32)

    me = lax.axis_index("turn")
    slot = lax.broadcasted_iota(jnp.int32, (slots, queries), 0)
    away = jnp.zeros_like(slot)
    for k, (axis, bit, _) in enumerate(steps):
        if axis == "turn":
            away = away + ((slot >> k) & 1) * bit
    owner = jnp.bitwise_xor(away, me)
    path = owner == me
    at = me
    for _ in range(turns - 1):
        at = jnp.where(at >= 0, parents_ref[jnp.maximum(at, 0)], -1)
        path = path | (owner == at)
    turn_bias = jnp.where(path, 0.0, masked_score).astype(f32)
    for r in range(trunk_rows + turn_rows):
        piece = jnp.zeros_like(turn_bias) if r < trunk_rows else turn_bias
        bias_ref[r * slots:(r + 1) * slots] = piece

    for ref, sem in ((kv_ref, 2), (q_ref, 3), (do_ref, 4)):
        pltpu.make_async_copy(ref, ref, sems.at[sem]).wait()


def head_chunks(first, last, per_group, per):
    for group in range(first, last):
        for lo in range(group * per_group, (group + 1) * per_group, per):
            yield group, lo


def own_kernel(first_group, per_group, per, q_ref, do_ref, kv_ref, bias_ref, e_ref, dp_ref, stat_ref):
    queries = bias_ref.shape[0]
    groups = e_ref.shape[1] // (queries * per_group)
    bias = jnp.concatenate([bias_ref[...]] * per, axis=1)
    base = first_group * per_group
    for group, lo in head_chunks(first_group, first_group + groups, per_group, per):
        heads = slice(lo * queries, (lo + per) * queries)
        span = slice((lo - base) * queries, (lo - base + per) * queries)
        s = dot(kv_ref[0, group], q_ref[heads], NT) + bias
        top = jnp.max(s, axis=0, keepdims=True)
        e = jnp.exp2((s - top) * exp2_scale)
        dp = dot(kv_ref[1, group], do_ref[heads], NT)
        e_ref[:, span] = e
        dp_ref[:, span] = dp
        stat_ref[0:1, span] = top
        stat_ref[1:2, span] = jnp.sum(e, axis=0, keepdims=True)
        stat_ref[2:3, span] = jnp.sum(e * dp, axis=0, keepdims=True)


def shared_rows_of(shared_ref, rows, features, part, group):
    return jnp.concatenate(
        [
            shared_ref[:, pl.ds((2 * r + part) * features + group * HEAD_SIZE, HEAD_SIZE)]
            for r in range(rows)
        ],
        axis=0,
    )


def shared_kernel(
    trunk_rows, turn_rows, per_group, per, parts, near_ref, far_ref, q_ref, do_ref, bias_ref, *refs
):
    stat_refs, refs = refs[:parts], refs[parts:]
    shared_ref, w_ref, ds_ref, joined_ref, keep_ref, send_ref = refs
    queries = bias_ref.shape[1]
    slots = shared_ref.shape[0]
    shared_ref[:slots // 2] = near_ref[...]
    shared_ref[slots // 2:] = far_ref[...]
    rows = trunk_rows + turn_rows
    features = shared_ref.shape[1] // (2 * rows)
    groups = features // HEAD_SIZE
    half = slots // 2
    shared = rows * slots
    bias = jnp.concatenate([bias_ref[...]] * per, axis=1)

    for group in range(groups):
        keys = shared_rows_of(shared_ref, rows, features, 0, group)
        values = shared_rows_of(shared_ref, rows, features, 1, group)
        first, last = group * per_group, (group + 1) * per_group
        all_w, all_ds = [], []
        for lo in range(first, last, per):
            heads = slice(lo * queries, (lo + per) * queries)
            part, place = divmod(lo, groups * per_group // parts)
            stat_ref = stat_refs[part]
            stat = slice(place * queries, (place + per) * queries)
            own_top = stat_ref[0:1, stat]
            s = dot(keys, q_ref[heads], NT) + bias
            top = jnp.maximum(jnp.max(s, axis=0, keepdims=True), own_top)
            e = jnp.exp2((s - top) * exp2_scale)
            shrink = jnp.exp2((own_top - top) * exp2_scale)
            dp = dot(values, do_ref[heads], NT)
            total = jnp.sum(e, axis=0, keepdims=True) + shrink * stat_ref[1:2, stat]
            inverse = 1.0 / total
            delta = inverse * (
                jnp.sum(e * dp, axis=0, keepdims=True) + shrink * stat_ref[2:3, stat]
            )
            p = e * inverse
            w = p.astype(bf16)
            ds = (p * (dp - delta)).astype(bf16)
            for h in range(per):
                place = slice((lo + h) * shared, (lo + h + 1) * shared)
                w_ref[place] = w[:, h * queries:(h + 1) * queries]
                ds_ref[place] = ds[:, h * queries:(h + 1) * queries]
            all_w.append(w)
            all_ds.append(ds)
            joined_ref[0:1, heads] = shrink * inverse
            joined_ref[1:2, heads] = delta
        heads = slice(first * queries, last * queries)
        dk = dot(jnp.concatenate(all_ds, axis=1), q_ref[heads], NN) * softmax_scale
        dv = dot(jnp.concatenate(all_w, axis=1), do_ref[heads], NN)
        for part, grad in ((0, dk), (1, dv)):
            for r in range(rows):
                at_lane = pl.ds((2 * r + part) * features + group * HEAD_SIZE, HEAD_SIZE)
                keep_ref[:, at_lane] = grad[r * slots:r * slots + half]
                send_ref[:, at_lane] = grad[r * slots + half:(r + 1) * slots].astype(bf16)


def back_kernel(
    group, place, rows, per_group, per, aliased, q_ref, do_ref, kv_ref, shared_ref, ws_ref, dss_ref, joined_ref,
    e_ref, dp_ref, *refs,
):
    out_ref, dq_ref, dkv_ref, w_ref, ds_ref = refs[aliased:]
    queries = kv_ref.shape[2]
    features = kv_ref.shape[1] * HEAD_SIZE
    shared = shared_ref.shape[0] * rows

    def turned(part):
        before = shared_rows_of(shared_ref, rows, features, part, group)
        return jnp.concatenate([before, kv_ref[part, group]], axis=0).T

    keys_t, values_t = turned(0), turned(1)

    def all_rows(ref, head, own):
        before = [ref[(head + h) * shared:(head + h + 1) * shared] for h in range(per)]
        return jnp.concatenate([jnp.concatenate(before, axis=1), own], axis=0)

    def unstack(ref, lo, value):
        back = value.T
        for h in range(per):
            ref[:, (lo + h) * HEAD_SIZE:(lo + h + 1) * HEAD_SIZE] = back[h * queries:(h + 1) * queries]

    for lo in range(0, per_group, per):
        head = group * per_group + lo
        span = slice(lo * queries, (lo + per) * queries)
        stored = slice((place + lo) * queries, (place + lo + per) * queries)
        whole = slice(head * queries, (head + per) * queries)
        p = e_ref[:, stored] * joined_ref[0:1, whole]
        w = p.astype(bf16)
        ds = (p * (dp_ref[:, stored] - joined_ref[1:2, whole])).astype(bf16)
        w_ref[:, span] = w
        ds_ref[:, span] = ds
        o_t = dot(values_t, all_rows(ws_ref, head, w), NN)
        unstack(out_ref, lo, o_t.astype(bf16))
        dq_t = dot(keys_t, all_rows(dss_ref, head, ds), NN) * softmax_scale
        unstack(dq_ref, lo, dq_t.astype(bf16))
    heads = slice(group * per_group * queries, (group + 1) * per_group * queries)
    dk = dot(ds_ref[...], q_ref[heads], NN) * softmax_scale
    dv = dot(w_ref[...], do_ref[heads], NN)
    dkv_ref[0] = dk.astype(bf16)
    dkv_ref[1] = dv.astype(bf16)


def pack_kernel(trunk_rows, features, trunk_hbm, turn_hbm, out_ref, trunk_ref, turn_ref, sems):
    copies = [
        pltpu.make_async_copy(trunk_hbm, trunk_ref, sems.at[0]),
        pltpu.make_async_copy(turn_hbm, turn_ref, sems.at[1]),
    ]
    for copy in copies:
        copy.start()
    for copy in copies:
        copy.wait()
    rows = out_ref.shape[1] // (2 * features)
    for r in range(rows):
        for part in range(2):
            lane = (2 * r + part) * features
            if r < trunk_rows:
                piece = trunk_ref[r, part:part + 1, :]
            else:
                piece = turn_ref[part, r - trunk_rows:r - trunk_rows + 1, :]
            out_ref[:, lane:lane + features] = piece


def finish_kernel(trunk_rows, features, total_ref, last_ref, trunk_ref, turn_ref):
    total = (total_ref[...] + last_ref[...].astype(f32)).astype(bf16)
    rows = total.shape[1] // (2 * features)
    for r in range(rows):
        for part in range(2):
            lane = (2 * r + part) * features
            piece = total[:, lane:lane + features]
            if r < trunk_rows:
                trunk_ref[r, part:part + 1, :] = piece
            else:
                turn_ref[part, r - trunk_rows:r - trunk_rows + 1, :] = piece


params = pltpu.CompilerParams(vmem_limit_bytes=16 * 2 ** 20)


def on_device(mesh, query, branch_kv, turn_kv, trunk_kv, grad_out, lengths, parents):
    steps = exchange_steps(mesh)
    slots = 2 ** len(steps)
    queries, width = query.shape
    features = branch_kv.shape[2]
    groups = features // HEAD_SIZE
    per_group = width // features
    per = 2 if per_group % 2 == 0 else 1
    parts = 2 if groups % 2 == 0 else 1
    trunk_rows, turn_rows = trunk_kv.shape[1], turn_kv.shape[1]
    rows = trunk_rows + turn_rows
    flat = rows * 2 * features
    spread = queries * per_group
    shape = jax.ShapeDtypeStruct

    heads = groups * per_group
    q, do, kv, own_bias, bias = pl.pallas_call(
        functools.partial(load_kernel, steps, trunk_rows, turn_rows, mesh.shape["turn"]),
        in_specs=[hbm] * 5,
        out_specs=[vmem] * 5,
        out_shape=[
            shape((heads * queries, HEAD_SIZE), bf16),
            shape((heads * queries, HEAD_SIZE), bf16),
            shape((2, groups, queries, HEAD_SIZE), bf16),
            shape((queries, queries), f32),
            shape((slots * rows, queries), f32),
        ],
        scratch_shapes=[
            pltpu.SMEM(lengths.shape, jnp.int32),
            pltpu.SMEM(parents.shape, jnp.int32),
            pltpu.SemaphoreType.DMA((5,)),
        ],
        compiler_params=params,
        name="load",
    )(*[in_hbm(x) for x in (query, grad_out, branch_kv, lengths, parents)])

    own_parts = []
    for part in range(parts):
        own_parts.append(pl.pallas_call(
            functools.partial(own_kernel, part * groups // parts, per_group, per),
            in_specs=[vmem] * 4,
            out_specs=[vmem] * 3,
            out_shape=[
                shape((queries, spread * groups // parts), f32),
                shape((queries, spread * groups // parts), f32),
                shape((8, spread * groups // parts), f32),
            ],
            compiler_params=params,
        )(q, do, kv, own_bias))

    near = pl.pallas_call(
        functools.partial(pack_kernel, trunk_rows, features),
        in_specs=[hbm] * 2,
        out_specs=vmem,
        out_shape=shape((1, flat), bf16),
        scratch_shapes=[
            pltpu.VMEM((trunk_rows, 2, features), bf16),
            pltpu.VMEM(turn_kv.shape, bf16),
            pltpu.SemaphoreType.DMA((2,)),
        ],
        compiler_params=params,
        name="pack",
    )(in_hbm(jnp.swapaxes(trunk_kv, 0, 1)), in_hbm(turn_kv))
    for k, step in enumerate(steps):
        if k:
            near = jnp.concatenate([near, far], axis=0)
        far = swap(near, step)

    held, shared_w, shared_ds, joined, total, send = pl.pallas_call(
        functools.partial(shared_kernel, trunk_rows, turn_rows, per_group, per, parts),
        in_specs=[vmem] * (5 + parts),
        out_specs=[vmem] * 6,
        out_shape=[
            shape((slots, flat), bf16),
            shape((heads * slots * rows, queries), bf16),
            shape((heads * slots * rows, queries), bf16),
            shape((8, spread * groups), f32),
            shape((slots // 2, flat), f32),
            shape((slots // 2, flat), bf16),
        ],
        compiler_params=params,
        name="shared",
    )(near, far, q, do, bias, *[p[2] for p in own_parts])

    made = ()
    block = lambda g: pl.BlockSpec((queries, spread_width), lambda i: (0, g))
    spread_width = width // groups
    for group in range(groups):
        part, place = divmod(group, groups // parts)
        e, dp, _ = own_parts[part]
        made = pl.pallas_call(
            functools.partial(back_kernel, group, place * per_group, rows, per_group, per, len(made)),
            grid=(1,),
            in_specs=[vmem] * 9 + [hbm] * len(made),
            out_specs=[
                block(group), block(group),
                pl.BlockSpec((2, queries, HEAD_SIZE), lambda i, g=group: (0, 0, g)),
            ],
            out_shape=[
                shape(query.shape, bf16), shape(query.shape, bf16), shape(branch_kv.shape, bf16)
            ],
            scratch_shapes=[pltpu.VMEM((queries, spread), bf16)] * 2,
            input_output_aliases={9 + i: i for i in range(len(made))},
            compiler_params=params,
        )(q, do, kv, held, shared_w, shared_ds, joined, e, dp, *made)

    for k in reversed(range(len(steps))):
        came = swap(send, steps[k])
        if k:
            total = total + came.astype(f32)
            half = total.shape[0] // 2
            send, total = total[half:].astype(bf16), total[:half]
    grad_trunk, grad_turn = pl.pallas_call(
        functools.partial(finish_kernel, trunk_rows, features),
        in_specs=[vmem] * 2,
        out_shape=[shape((trunk_rows, 2, features), bf16), shape(turn_kv.shape, bf16)],
        compiler_params=params,
        name="finish",
    )(total, came)
    return (*made, grad_turn, jnp.swapaxes(grad_trunk, 0, 1))


def solution(mesh):
    everywhere = ("parts", "turn", "branch")
    by_row = P(everywhere, None)
    by_middle = P(None, everywhere, None)

    def layer(*args):
        return on_device(mesh, *args)

    return jax.shard_map(
        layer,
        mesh=mesh,
        in_specs=(by_row, by_middle, by_middle, by_middle, by_row, by_row, P("parts")),
        out_specs=(by_row, by_row, by_middle, by_middle, by_middle),
        check_vma=False,
    )
```

time: 43.9 us -> 37.6 us (0.86)
  local copies, waits for them, and re-layouts: 5.54 us -> 0.06 us
  Pallas kernels: 11.4 us -> 10.7 us
    unnamed x20 -> x0, local copies, waits for them, and re-layouts: 5.48 us -> none
    pallas_call x4 -> x2, Pallas kernels: 3.64 us -> 1.07 us  [on_device(): pl.pallas_call(functools.partial(own_kernel, part * groups // parts, per_...]
    pallas_call x1 -> x2, Pallas kernels: 2.13 us -> 3.24 us  [the longest x1 1.67 us: on_device(): pl.pallas_call(functools.partial(load_kernel, steps, trunk_rows, turn_row...]
    pallas_call x1, Pallas kernels: 0.01 us -> 0.73 us  [on_device(): pl.pallas_call(functools.partial(pack_kernel, trunk_rows, features), in_s...]
  transfers between devices with their start and end apart: 8 -> 8, of which waited for: 6 -> 6; matrix products, arithmetic and copies ran while one was open for 0% -> 0% of each run, Pallas kernels for 20% -> 21%
where the time goes in v3:
time: 37.6 us; the launch traced here: 37.3 us
  starting transfers between devices  15.5 us (41%)
  Pallas kernels  10.7 us (28%)
  waiting for transfers between devices  10.1 us (27%)
  between operations  0.74 us (2%)
    ppermute x8, starting transfers between devices, swap(): return lax.ppermute(x, axis, [(i, i ^ bit) for i in range(size)])  15.5 us
    ppermute x8, waiting for transfers between devices, swap(): return lax.ppermute(x, axis, [(i, i ^ bit) for i in range(size)])  10.1 us
    pallas_call x4, Pallas kernels, on_device(): pl.pallas_call(functools.partial(back_kernel, group, place * per_group, r...  5.06 us
    pallas_call x1, Pallas kernels, on_device(): pl.pallas_call(functools.partial(load_kernel, steps, trunk_rows, turn_row...  1.67 us
    pallas_call x1, Pallas kernels, on_device(): pl.pallas_call(functools.partial(shared_kernel, trunk_rows, turn_rows, pe...  1.57 us
    pallas_call x2, Pallas kernels, on_device(): pl.pallas_call(functools.partial(own_kernel, part * groups // parts, per_...  1.07 us
  transfers between devices with their start and end apart: 8, of which 6 were waited for; matrix products, arithmetic and copies ran while one was open for 0% of the time, Pallas kernels for 21%

profile of v3, /device:TPU:0, one launch (start us, length us, event | category | flops | bytes accessed | tf_op | source)
XLA Modules:
  0.0 37.3 jit_solution(2616255437306363654)
XLA Ops:
  0.6 0.7 %pack.1 = bf16[1,3072]{1,0:T(2,128)(2,1)S(1)} custom-call(bf16[1,2,512]{2,1,0:T(2,128)(2,1)} %bitcast.2, bf16[2,2,512]{2,1,0:T(2,128)(2,1)} %turn_hbm.1), custom_call_target="tpu_custom_call" | custom-call | tf_op jit(solution)/shard_map/pack/pallas_call | solution.py:329
  1.4 4.1 %collective-permute-start = (bf16[1,3072]{1,0:T(2,128)(2,1)S(1)}, bf16[1,3072]{1,0:T(2,128)(2,1)S(1)}, u32[]{:S(2)}, u32[]{:S(2)}) collective-permute-start(bf16[1,3072]{1,0:T(2,128)(2,1)S(1)} %pack.1), channel_id=1, source_target_pairs={{0,2},{1,3},{2,0},{3,1},{4,6},{5,7},{6,4},{7,5},{8,10},{9,11},{10,... | collective-permute-start | bytes 18440 | tf_op jit(solution)/shard_map/ppermute | solution.py:38
  5.5 1.7 %collective-permute-done = bf16[1,3072]{1,0:T(2,128)(2,1)S(1)} collective-permute-done((bf16[1,3072]{1,0:T(2,128)(2,1)S(1)}, bf16[1,3072]{1,0:T(2,128)(2,1)S(1)}, u32[]{:S(2)}, u32[]{:S(2)}) %collective-permute-start) | collective-permute-done | bytes 6176 | tf_op jit(solution)/shard_map/ppermute | solution.py:38
  7.2 2.0 %collective-permute-start.1 = (bf16[2,3072]{1,0:T(2,128)(2,1)S(1)}, bf16[2,3072]{1,0:T(2,128)(2,1)S(1)}, u32[]{:S(2)}, u32[]{:S(2)}) collective-permute-start(bf16[2,3072]{1,0:T(2,128)(2,1)S(1)} %pad_maximum_fusion.2), channel_id=1, source_target_pairs={{0,1},{1,0},{2,3},{3,2},{4,5},{5,4},{6,7},{7,6},{8,9},{9,8},{10,11... | collective-permute-start | bytes 36872 | tf_op jit(solution)/shard_map/ppermute | solution.py:38
  9.2 1.8 %collective-permute-done.1 = bf16[2,3072]{1,0:T(2,128)(2,1)S(1)} collective-permute-done((bf16[2,3072]{1,0:T(2,128)(2,1)S(1)}, bf16[2,3072]{1,0:T(2,128)(2,1)S(1)}, u32[]{:S(2)}, u32[]{:S(2)}) %collective-permute-start.1) | collective-permute-done | bytes 12320 | tf_op jit(solution)/shard_map/ppermute | solution.py:38
  11.0 1.9 %collective-permute-start.2 = (bf16[4,3072]{1,0:T(4,128)(2,1)S(1)}, bf16[4,3072]{1,0:T(4,128)(2,1)S(1)}, u32[]{:S(2)}, u32[]{:S(2)}) collective-permute-start(bf16[4,3072]{1,0:T(4,128)(2,1)S(1)} %pad_maximum_fusion.1), channel_id=1, source_target_pairs={{0,8},{4,12},{8,0},{12,4},{1,9},{5,13},{9,1},{13,5},{2,10},{6,14},... | collective-permute-start | bytes 73736 | tf_op jit(solution)/shard_map/ppermute | solution.py:38
  12.9 2.0 %collective-permute-done.2 = bf16[4,3072]{1,0:T(4,128)(2,1)S(1)} collective-permute-done((bf16[4,3072]{1,0:T(4,128)(2,1)S(1)}, bf16[4,3072]{1,0:T(4,128)(2,1)S(1)}, u32[]{:S(2)}, u32[]{:S(2)}) %collective-permute-start.2) | collective-permute-done | bytes 24608 | tf_op jit(solution)/shard_map/ppermute | solution.py:38
  14.9 0.1 pad_maximum_fusion.near_ref
  15.0 0.1 collective-permute-start.3
  15.1 1.7 %load.1 = (bf16[4096,128]{1,0:T(8,128)(2,1)S(1)}, bf16[4096,128]{1,0:T(8,128)(2,1)S(1)}, bf16[2,4,128,128]{3,2,1,0:T(8,128)(2,1)S(1)}, f32[128,128]{1,0:T(8,128)S(1)}, f32[48,128]{1,0:T(8,128)S(1)}) custom-call(bf16[128,4096]{1,0:T(8,128)(2,1)} %q_hbm.1, bf16[128,4096]{1,0:T(8,128)(2,1)} %do_hbm.1, bf16[2,128,512]{2,1,0:T(8,128)(2,1)} %kv_hbm.1, ...), custom_call_target="tpu_custom_call" | custom-call | tf_op jit(solution)/shard_map/load/pallas_call | solution.py:295
  16.7 0.5 %shard_map.111 = (f32[128,2048]{1,0:T(8,128)S(1)}, f32[128,2048]{1,0:T(8,128)S(1)}, f32[8,2048]{1,0:T(8,128)S(1)}) custom-call(bf16[4096,128]{1,0:T(8,128)(2,1)S(1)} %get-tuple-element.36.q_ref, bf16[4096,128]{1,0:T(8,128)(2,1)S(1)} %get-tuple-element.37.do_ref, bf16[2,4,128,128]{3,2,1,0:T(8,128)(2,1)S(1)} %get-tuple-element.38.kv_ref, ...), custom_call_target="tpu_custom_call" | custom-call | tf_op jit(solution)/shard_map/pallas_call | solution.py:317
  17.3 0.5 %shard_map.110 = (f32[128,2048]{1,0:T(8,128)S(1)}, f32[128,2048]{1,0:T(8,128)S(1)}, f32[8,2048]{1,0:T(8,128)S(1)}) custom-call(bf16[4096,128]{1,0:T(8,128)(2,1)S(1)} %get-tuple-element.36.q_ref, bf16[4096,128]{1,0:T(8,128)(2,1)S(1)} %get-tuple-element.37.do_ref, bf16[2,4,128,128]{3,2,1,0:T(8,128)(2,1)S(1)} %get-tuple-element.38.kv_ref, ...), custom_call_target="tpu_custom_call" | custom-call | tf_op jit(solution)/shard_map/pallas_call | solution.py:317
  17.8 0.0 collective-permute-done.3.far_ref
  17.8 1.6 %shared.1 = (bf16[16,3072]{1,0:T(8,128)(2,1)S(1)}, bf16[1536,128]{1,0:T(8,128)(2,1)S(1)}, bf16[1536,128]{1,0:T(8,128)(2,1)S(1)}, f32[8,4096]{1,0:T(8,128)S(1)}, ...) custom-call(bf16[8,3072]{1,0:T(8,128)(2,1)S(1)} %pad_maximum_fusion.near_ref, ...), custom_call_target="tpu_custom_call" | custom-call | tf_op jit(solution)/shard_map/shared/pallas_call | solution.py:347
  19.4 0.6 %collective-permute-start.4 = (bf16[8,3072]{1,0:T(8,128)(2,1)S(1)}, bf16[8,3072]{1,0:T(8,128)(2,1)S(1)}, u32[]{:S(2)}, u32[]{:S(2)}) collective-permute-start(bf16[8,3072]{1,0:T(8,128)(2,1)S(1)} %get-tuple-element.64), channel_id=1, source_target_pairs={{0,4},{4,0},{8,12},{12,8},{1,5},{5,1},{9,13},{13,9},{2,6},{6,2},{1... | collective-permute-start | bytes 147464 | tf_op jit(solution)/shard_map/ppermute | solution.py:38
  20.0 0.9 %collective-permute-done.4 = bf16[8,3072]{1,0:T(8,128)(2,1)S(1)} collective-permute-done((bf16[8,3072]{1,0:T(8,128)(2,1)S(1)}, bf16[8,3072]{1,0:T(8,128)(2,1)S(1)}, u32[]{:S(2)}, u32[]{:S(2)}) %collective-permute-start.4) | collective-permute-done | bytes 49184 | tf_op jit(solution)/shard_map/ppermute | solution.py:38
  20.9 1.9 %collective-permute-start.5 = (bf16[4,3072]{1,0:T(4,128)(2,1)S(1)}, bf16[4,3072]{1,0:T(4,128)(2,1)S(1)}, u32[]{:S(2)}, u32[]{:S(2)}) collective-permute-start(bf16[4,3072]{1,0:T(4,128)(2,1)S(1)} %slice.38), channel_id=1, source_target_pairs={{0,8},{4,12},{8,0},{12,4},{1,9},{5,13},{9,1},{13,5},{2,10},{6,14},... | collective-permute-start | bytes 73736 | tf_op jit(solution)/shard_map/ppermute | solution.py:38
  22.8 2.0 %collective-permute-done.5 = bf16[4,3072]{1,0:T(4,128)(2,1)S(1)} collective-permute-done((bf16[4,3072]{1,0:T(4,128)(2,1)S(1)}, bf16[4,3072]{1,0:T(4,128)(2,1)S(1)}, u32[]{:S(2)}, u32[]{:S(2)}) %collective-permute-start.5) | collective-permute-done | bytes 24608 | tf_op jit(solution)/shard_map/ppermute | solution.py:38
  24.8 2.0 %collective-permute-start.6 = (bf16[2,3072]{1,0:T(2,128)(2,1)S(1)}, bf16[2,3072]{1,0:T(2,128)(2,1)S(1)}, u32[]{:S(2)}, u32[]{:S(2)}) collective-permute-start(bf16[2,3072]{1,0:T(2,128)(2,1)S(1)} %slice.39), channel_id=1, source_target_pairs={{0,1},{1,0},{2,3},{3,2},{4,5},{5,4},{6,7},{7,6},{8,9},{9,8},{10,11... | collective-permute-start | bytes 36872 | tf_op jit(solution)/shard_map/ppermute | solution.py:38
  26.8 1.8 %collective-permute-done.6 = bf16[2,3072]{1,0:T(2,128)(2,1)S(1)} collective-permute-done((bf16[2,3072]{1,0:T(2,128)(2,1)S(1)}, bf16[2,3072]{1,0:T(2,128)(2,1)S(1)}, u32[]{:S(2)}, u32[]{:S(2)}) %collective-permute-start.6) | collective-permute-done | bytes 12320 | tf_op jit(solution)/shard_map/ppermute | solution.py:38
  28.6 3.0 %collective-permute-start.7 = (bf16[1,3072]{1,0:T(2,128)(2,1)S(1)}, bf16[1,3072]{1,0:T(2,128)(2,1)S(1)}, u32[]{:S(2)}, u32[]{:S(2)}) collective-permute-start(bf16[1,3072]{1,0:T(2,128)(2,1)S(1)} %slice.40), channel_id=1, source_target_pairs={{0,2},{1,3},{2,0},{3,1},{4,6},{5,7},{6,4},{7,5},{8,10},{9,11},{10,... | collective-permute-start | bytes 18440 | tf_op jit(solution)/shard_map/ppermute | solution.py:38
  31.6 1.3 %shard_map.112 = (bf16[128,4096]{1,0:T(8,128)(2,1)}, bf16[128,4096]{1,0:T(8,128)(2,1)}, bf16[2,128,512]{2,1,0:T(8,128)(2,1)}) custom-call(bf16[4096,128]{1,0:T(8,128)(2,1)S(1)} %get-tuple-element.36.q_ref, bf16[4096,128]{1,0:T(8,128)(2,1)S(1)} %get-tuple-element.37.do_ref, bf16[2,4,128,128]{3,2,1,0:T(8,128)(2,1)S(1)} %get-tuple-element.38.kv_ref, ...), custom_call_target="tpu_custom_call" | custom-call | tf_op jit(solution)/shard_map/pallas_call | solution.py:369
  32.9 1.3 %shard_map.113 = (bf16[128,4096]{1,0:T(8,128)(2,1)}, bf16[128,4096]{1,0:T(8,128)(2,1)}, bf16[2,128,512]{2,1,0:T(8,128)(2,1)}) custom-call(bf16[4096,128]{1,0:T(8,128)(2,1)S(1)} %get-tuple-element.36.q_ref, bf16[4096,128]{1,0:T(8,128)(2,1)S(1)} %get-tuple-element.37.do_ref, ...), custom_call_target="tpu_custom_call", output_to_operand_aliasing={{0}: (9, {}), {1}: (10, {}), {2}: (11, {})} | custom-call | tf_op jit(solution)/shard_map/pallas_call | solution.py:369
  34.1 1.3 %shard_map.114 = (bf16[128,4096]{1,0:T(8,128)(2,1)}, bf16[128,4096]{1,0:T(8,128)(2,1)}, bf16[2,128,512]{2,1,0:T(8,128)(2,1)}) custom-call(bf16[4096,128]{1,0:T(8,128)(2,1)S(1)} %get-tuple-element.36.q_ref, bf16[4096,128]{1,0:T(8,128)(2,1)S(1)} %get-tuple-element.37.do_ref, ...), custom_call_target="tpu_custom_call", output_to_operand_aliasing={{0}: (9, {}), {1}: (10, {}), {2}: (11, {})} | custom-call | tf_op jit(solution)/shard_map/pallas_call | solution.py:369
  35.4 1.3 %shard_map.115 = (bf16[128,4096]{1,0:T(8,128)(2,1)}, bf16[128,4096]{1,0:T(8,128)(2,1)}, bf16[2,128,512]{2,1,0:T(8,128)(2,1)}) custom-call(bf16[4096,128]{1,0:T(8,128)(2,1)S(1)} %get-tuple-element.36.q_ref, bf16[4096,128]{1,0:T(8,128)(2,1)S(1)} %get-tuple-element.37.do_ref, ...), custom_call_target="tpu_custom_call", output_to_operand_aliasing={{0}: (9, {}), {1}: (10, {}), {2}: (11, {})} | custom-call | tf_op jit(solution)/shard_map/pallas_call | solution.py:369
  36.7 0.0 collective-permute-done.7.last_ref
  36.7 0.6 %finish.1 = (bf16[1,2,512]{2,1,0:T(2,128)(2,1)}, bf16[2,2,512]{2,1,0:T(2,128)(2,1)}) custom-call(f32[1,3072]{1,0:T(1,128)S(1)} %slice.31.total_ref, bf16[1,3072]{1,0:T(2,128)(2,1)S(1)} %collective-permute-done.7.last_ref), custom_call_target="tpu_custom_call" | custom-call | tf_op jit(solution)/shard_map/finish/pallas_call | solution.py:391
  (9 shorter events, 0.2 us)
Async XLA Ops:
  1.4 5.8 %collective-permute-start = (bf16[1,3072]{1,0:T(2,128)(2,1)S(1)}, bf16[1,3072]{1,0:T(2,128)(2,1)S(1)}, u32[]{:S(2)}, u32[]{:S(2)}) collective-permute-start(bf16[1,3072]{1,0:T(2,128)(2,1)S(1)} %pack.1), channel_id=1, source_target_pairs={{0,2},{1,3},{2,0},{3,1},{4,6},{5,7},{6,4},{7,5},{8,10},{9,11},{10,... | collective-permute-start | bytes 18440 | tf_op jit(solution)/shard_map/ppermute | solution.py:38
  7.2 3.8 %collective-permute-start.1 = (bf16[2,3072]{1,0:T(2,128)(2,1)S(1)}, bf16[2,3072]{1,0:T(2,128)(2,1)S(1)}, u32[]{:S(2)}, u32[]{:S(2)}) collective-permute-start(bf16[2,3072]{1,0:T(2,128)(2,1)S(1)} %pad_maximum_fusion.2), channel_id=1, source_target_pairs={{0,1},{1,0},{2,3},{3,2},{4,5},{5,4},{6,7},{7,6},{8,9},{9,8},{10,11... | collective-permute-start | bytes 36872 | tf_op jit(solution)/shard_map/ppermute | solution.py:38
  11.0 3.9 %collective-permute-start.2 = (bf16[4,3072]{1,0:T(4,128)(2,1)S(1)}, bf16[4,3072]{1,0:T(4,128)(2,1)S(1)}, u32[]{:S(2)}, u32[]{:S(2)}) collective-permute-start(bf16[4,3072]{1,0:T(4,128)(2,1)S(1)} %pad_maximum_fusion.1), channel_id=1, source_target_pairs={{0,8},{4,12},{8,0},{12,4},{1,9},{5,13},{9,1},{13,5},{2,10},{6,14},... | collective-permute-start | bytes 73736 | tf_op jit(solution)/shard_map/ppermute | solution.py:38
  15.0 2.8 %collective-permute-start.3 = (bf16[8,3072]{1,0:T(8,128)(2,1)S(1)}, bf16[8,3072]{1,0:T(8,128)(2,1)S(1)}, u32[]{:S(2)}, u32[]{:S(2)}) collective-permute-start(bf16[8,3072]{1,0:T(8,128)(2,1)S(1)} %pad_maximum_fusion.near_ref), channel_id=1, source_target_pairs={{0,4},{4,0},{8,12},{12,8},{1,5},{5,1},{9,13},{13,9},{2,6},{6,2},{1... | collective-permute-start | bytes 147464 | tf_op jit(solution)/shard_map/ppermute | solution.py:38
  19.4 1.4 %collective-permute-start.4 = (bf16[8,3072]{1,0:T(8,128)(2,1)S(1)}, bf16[8,3072]{1,0:T(8,128)(2,1)S(1)}, u32[]{:S(2)}, u32[]{:S(2)}) collective-permute-start(bf16[8,3072]{1,0:T(8,128)(2,1)S(1)} %get-tuple-element.64), channel_id=1, source_target_pairs={{0,4},{4,0},{8,12},{12,8},{1,5},{5,1},{9,13},{13,9},{2,6},{6,2},{1... | collective-permute-start | bytes 147464 | tf_op jit(solution)/shard_map/ppermute | solution.py:38
  20.9 3.9 %collective-permute-start.5 = (bf16[4,3072]{1,0:T(4,128)(2,1)S(1)}, bf16[4,3072]{1,0:T(4,128)(2,1)S(1)}, u32[]{:S(2)}, u32[]{:S(2)}) collective-permute-start(bf16[4,3072]{1,0:T(4,128)(2,1)S(1)} %slice.38), channel_id=1, source_target_pairs={{0,8},{4,12},{8,0},{12,4},{1,9},{5,13},{9,1},{13,5},{2,10},{6,14},... | collective-permute-start | bytes 73736 | tf_op jit(solution)/shard_map/ppermute | solution.py:38
  24.8 3.8 %collective-permute-start.6 = (bf16[2,3072]{1,0:T(2,128)(2,1)S(1)}, bf16[2,3072]{1,0:T(2,128)(2,1)S(1)}, u32[]{:S(2)}, u32[]{:S(2)}) collective-permute-start(bf16[2,3072]{1,0:T(2,128)(2,1)S(1)} %slice.39), channel_id=1, source_target_pairs={{0,1},{1,0},{2,3},{3,2},{4,5},{5,4},{6,7},{7,6},{8,9},{9,8},{10,11... | collective-permute-start | bytes 36872 | tf_op jit(solution)/shard_map/ppermute | solution.py:38
  28.6 8.1 %collective-permute-start.7 = (bf16[1,3072]{1,0:T(2,128)(2,1)S(1)}, bf16[1,3072]{1,0:T(2,128)(2,1)S(1)}, u32[]{:S(2)}, u32[]{:S(2)}) collective-permute-start(bf16[1,3072]{1,0:T(2,128)(2,1)S(1)} %slice.40), channel_id=1, source_target_pairs={{0,2},{1,3},{2,0},{3,1},{4,6},{5,7},{6,4},{7,5},{8,10},{9,11},{10,... | collective-permute-start | bytes 18440 | tf_op jit(solution)/shard_map/ppermute | solution.py:38
